TPU v7x, 512 devices: a whole 4x8x8 slice. The times are simulated.
512 devices in a mesh: mapx: 32 (over x, z), mapy: 8 (over y), layer: 2 (over core).
Axes of the slice: x: 4, y: 8, z: 8, core: 2. Of those that a mesh axis runs over, the one named last changes fastest.
Arguments:
- old_state: float32 [32, 8, 2, 6, 8192], P('mapx', 'mapy', 'layer'), as said below
- send_blocks: int32 [32, 8, 2, 10, 16], P('mapx', 'mapy', 'layer'), may hold values from 0 to 63
- node_slots: int32 [32, 8, 2, 4, 512], P('mapx', 'mapy', 'layer'), may hold values from 0 to 20479, as said below
- node_weights: float32 [32, 8, 2, 4, 512], P('mapx', 'mapy', 'layer'), as said below
- front_mask: int32 [32, 8, 2, 512], P('mapx', 'mapy', 'layer'), may hold values 0 or 1
- halo_lists: int32 [32, 8, 2, 6, 256], P('mapx', 'mapy', 'layer'), may hold values from 0 to 511
- elem_nodes: int32 [32, 8, 2, 4, 2560], P('mapx', 'mapy', 'layer'), may hold values from 0 to 2047
- shape_grads: float32 [32, 8, 2, 12, 2560], P('mapx', 'mapy', 'layer'), as said below
- elem_volume: float32 [32, 8, 2, 2560], P('mapx', 'mapy', 'layer'), may hold values from 0.5 to 2
Outputs:
- new_state: float32 [32, 8, 2, 6, 512], P('mapx', 'mapy', 'layer')
- residual: float32 [32, 8, 2, 4, 512], P('mapx', 'mapy', 'layer')
Inputs may be any that keep to these rules, and one draw needn't show every extreme that they name: `send_blocks`: each entry names one of the sender's old blocks; a block may go to several peers or twice to one. `node_slots`: indexes the received nodes, ordered by source (mapx offset plus 2, times 2, plus layer index), then slot, then node in the block; only sources inside the device grid are named. `node_weights`: Positive; the four weights of a node sum to one. `halo_lists`: owned nodes kept as ghosts by the neighbour in direction k. `elem_nodes`: local numbering: the owned nodes first, then 256 ghosts for each of the six directions in order. `shape_grads`: the four gradients of an element sum to zero. `old_state`: rows 0 to 3 velocity and pressure, row 4 temperature in [-1, 0], row 5 damage in [0, 0.9].
All inputs are finite; a program needn't handle non-finite values. No bound on the sum of `front_mask` on one device may be relied on, other than what follows from the above.
Results may differ from a plain program's by a relative error of at most 0.00002.
Values sent between devices are 32-bit elements; how exact they have to be, the bound alone decides.
A program may use at most 64 MiB of HBM per device.

v0:
```python
import jax
import jax.numpy as jnp
from jax import lax
from jax.sharding import PartitionSpec as P

BLOCK = 128
REACH = 2


ocean_temp = 0.0
strain_reg = 0.01
gravity = 0.5


def passed_along(value, axis, steps):
    count = lax.axis_size(axis)
    first, last = (max(0, -steps), min(count, count - steps))
    return lax.ppermute(value, axis, [(source, source + steps) for source in range(first, last)])


def element_residual(node_table, elem_nodes, shape_grads, elem_volume):
    values = jnp.take(node_table, elem_nodes, axis=1)
    grads = shape_grads.reshape(4, 3, -1)
    velgrad = jnp.sum(values[:3, :, None, :] * grads[None, :, :, :], axis=1)
    strain = 0.5 * (velgrad + jnp.transpose(velgrad, (1, 0, 2)))
    second = 0.5 * jnp.sum(strain * strain, axis=(0, 1))
    means = jnp.mean(values[3:], axis=1)
    viscosity = 0.5 * (1.0 - means[2]) * jnp.exp(-means[1]) * (second + strain_reg) ** (-1.0 / 3.0)
    stress = 2.0 * viscosity * strain - means[0] * jnp.eye(3, dtype=strain.dtype)[:, :, None]
    momentum = elem_volume * jnp.sum(stress[None, :, :, :] * grads[:, None, :, :], axis=2)
    upward = jnp.array([0.0, 0.0, 1.0], dtype=momentum.dtype)
    momentum = momentum + (0.25 * gravity * elem_volume)[None, None, :] * upward[None, :, None]
    divergence = velgrad[0, 0] + velgrad[1, 1] + velgrad[2, 2]
    continuity = 0.25 * elem_volume * divergence
    cont_rows = jnp.broadcast_to(continuity[None, None, :], (4, 1, continuity.shape[0]))
    return jnp.concatenate([momentum, cont_rows], axis=1)


def usable(shift_by, count_y, count_l, pos_y, pos_l):
    if abs(shift_by) == count_y * count_l:
        return jnp.float32(1.0)
    if shift_by == count_l:
        inside = pos_y >= 1
    elif shift_by == -count_l:
        inside = pos_y <= count_y - 2
    elif shift_by == 1:
        inside = pos_l >= 1
    else:
        inside = pos_l <= count_l - 2
    return jnp.where(inside, 1.0, 0.0).astype(jnp.float32)


def fetch_ghost(portion, shift_by):
    return passed_along(portion, ("mapx", "mapy", "layer"), shift_by)


def return_sums(portion, shift_by):
    return passed_along(portion, ("mapx", "mapy", "layer"), shift_by)


def move_column(portion, offset):
    if offset == 0:
        return portion
    return passed_along(portion, "mapx", -offset)


def sort_layers(portion):
    return lax.all_to_all(portion, "layer", split_axis=2, concat_axis=2, tiled=True)


def per_device(
    old_state,
    send_blocks,
    node_slots,
    node_weights,
    front_mask,
    halo_lists,
    elem_nodes,
    shape_grads,
    elem_volume,
):
    spread = 2 * REACH + 1
    old_values = old_state[0, 0, 0].reshape(6, -1, BLOCK)
    block_ids = send_blocks[0, 0, 0]
    count_layer = lax.axis_size("layer")
    outgoing = jnp.take(old_values, block_ids, axis=1)
    outgoing = outgoing.reshape(6, spread, count_layer, block_ids.shape[1], BLOCK)
    sorted_blocks = sort_layers(outgoing)
    columns = [
        move_column(sorted_blocks[:, spread - 1 - source], source - REACH)
        for source in range(spread)
    ]
    received = jnp.stack(columns, axis=1)
    received = received.reshape(6, -1)
    gathered = jnp.take(received, node_slots[0, 0, 0], axis=1)
    interpolated = jnp.sum(gathered * node_weights[0, 0, 0][None], axis=1)
    temp_row = (jnp.arange(6) == 4)[:, None]
    new_state = jnp.where(temp_row & (front_mask[0, 0, 0] == 1)[None, :], ocean_temp, interpolated)
    count_y = lax.axis_size("mapy")
    count_l = lax.axis_size("layer")
    pos_y = lax.axis_index("mapy")
    pos_l = lax.axis_index("layer")
    offsets = (count_y * count_l, -count_y * count_l, count_l, -count_l, 1, -1)
    halos = halo_lists[0, 0, 0]
    owned = new_state.shape[1]
    pieces = [new_state]
    for index in range(6):
        portion = jnp.take(new_state, halos[index], axis=1)
        arrived = fetch_ghost(portion, offsets[index])
        pieces.append(arrived * usable(offsets[index], count_y, count_l, pos_y, pos_l))
    node_table = jnp.concatenate(pieces, axis=1)
    width = node_table.shape[1]
    ghost_count = halos.shape[1]
    nodes = elem_nodes[0, 0, 0]
    contrib = element_residual(node_table, nodes, shape_grads[0, 0, 0], elem_volume[0, 0, 0])
    flat_terms = jnp.transpose(contrib, (0, 2, 1)).reshape(-1, 4)
    assembled = jax.ops.segment_sum(flat_terms, nodes.reshape(-1), num_segments=width).T
    residual = assembled[:, :owned]
    returned = []
    for index in range(6):
        start = owned + index * ghost_count
        portion = assembled[:, start : start + ghost_count]
        arrived = return_sums(portion, -offsets[index])
        returned.append(arrived * usable(-offsets[index], count_y, count_l, pos_y, pos_l))
    all_returned = jnp.concatenate(returned, axis=1)
    residual = (
        residual + jax.ops.segment_sum(all_returned.T, halos.reshape(-1), num_segments=owned).T
    )
    return (new_state[None, None, None], residual[None, None, None])


def solution(mesh):
    return jax.shard_map(
        per_device,
        mesh=mesh,
        in_specs=(
            P("mapx", "mapy", "layer", None, None),
            P("mapx", "mapy", "layer", None, None),
            P("mapx", "mapy", "layer", None, None),
            P("mapx", "mapy", "layer", None, None),
            P("mapx", "mapy", "layer", None),
            P("mapx", "mapy", "layer", None, None),
            P("mapx", "mapy", "layer", None, None),
            P("mapx", "mapy", "layer", None, None),
            P("mapx", "mapy", "layer", None),
        ),
        out_specs=(P("mapx", "mapy", "layer", None, None), P("mapx", "mapy", "layer", None, None)),
        check_vma=False,
    )
```

profile of v0, /device:TPU:6, one launch (start us, length us, event | category | flops | bytes accessed | tf_op | source)
XLA Modules:
  0.0 242.8 jit_solution(14053429904828143759)
XLA Ops:
  0.7 1.1 copy.165
  1.8 0.7 fusion.12
  2.5 0.1 reshape.338
  2.6 0.8 gather_fusion
  3.5 0.1 copy.166
  3.6 0.7 compare_and_fusion.1
  4.3 0.1 broadcast_select_fusion
  4.4 4.1 %all_to_all.5 = f32[6,5,2,16,128]{4,3,1,0,2:T(8,128)S(1)} all-to-all(f32[6,5,2,16,128]{4,3,1,0,2:T(8,128)S(1)} %copy.167), channel_id=1, replica_groups=mesh['mapx'=32,'mapy'=8,'layer'=2] {'layer'}, dimensions={2} | all-to-all | bytes 983040 | tf_op jit(solution)/shard_map/all_to_all | solution.py:68
  8.6 6.1 %collective-permute-start = (f32[6,2,16,128]{3,2,1,0:T(8,128)S(1)}, f32[6,2,16,128]{3,2,1,0:T(8,128)S(1)}, u32[]{:S(2)}, u32[]{:S(2)}) collective-permute-start(f32[6,2,16,128]{3,2,1,0:T(8,128)S(1)} %copy.168), channel_id=1, source_target_pairs={{0,32},{16,48},{32,64},{48,80},{64,96},{80,112},{96,128},{112,144}... | collective-permute-start | bytes 294920 | tf_op jit(solution)/shard_map/ppermute | solution.py:18
  14.7 4.3 %collective-permute-start.1 = (f32[6,2,16,128]{3,2,1,0:T(8,128)S(1)}, f32[6,2,16,128]{3,2,1,0:T(8,128)S(1)}, u32[]{:S(2)}, u32[]{:S(2)}) collective-permute-start(f32[6,2,16,128]{3,2,1,0:T(8,128)S(1)} %copy.170), channel_id=1, source_target_pairs={{0,16},{16,32},{32,48},{48,64},{64,80},{80,96},{96,112},{112,128},... | collective-permute-start | bytes 294920 | tf_op jit(solution)/shard_map/ppermute | solution.py:18
  19.4 0.3 reduce.4
  20.1 2.9 %collective-permute-done = f32[6,2,16,128]{3,2,1,0:T(8,128)S(1)} collective-permute-done((f32[6,2,16,128]{3,2,1,0:T(8,128)S(1)}, f32[6,2,16,128]{3,2,1,0:T(8,128)S(1)}, u32[]{:S(2)}, u32[]{:S(2)}) %collective-permute-start) | collective-permute-done | bytes 98336 | tf_op jit(solution)/shard_map/ppermute | solution.py:18
  23.0 4.1 %collective-permute-done.1 = f32[6,2,16,128]{3,2,1,0:T(8,128)S(1)} collective-permute-done((f32[6,2,16,128]{3,2,1,0:T(8,128)S(1)}, f32[6,2,16,128]{3,2,1,0:T(8,128)S(1)}, u32[]{:S(2)}, u32[]{:S(2)}) %collective-permute-start.1) | collective-permute-done | bytes 98336 | tf_op jit(solution)/shard_map/ppermute | solution.py:18
  27.1 3.4 %collective-permute-start.2 = (f32[6,2,16,128]{3,2,1,0:T(8,128)S(1)}, f32[6,2,16,128]{3,2,1,0:T(8,128)S(1)}, u32[]{:S(2)}, u32[]{:S(2)}) collective-permute-start(f32[6,2,16,128]{3,2,1,0:T(8,128)S(1)} %copy.172), channel_id=1, source_target_pairs={{16,0},{32,16},{48,32},{64,48},{80,64},{96,80},{112,96},{128,112},... | collective-permute-start | bytes 294920 | tf_op jit(solution)/shard_map/ppermute | solution.py:18
  30.6 3.6 %collective-permute-start.3 = (f32[6,2,16,128]{3,2,1,0:T(8,128)S(1)}, f32[6,2,16,128]{3,2,1,0:T(8,128)S(1)}, u32[]{:S(2)}, u32[]{:S(2)}) collective-permute-start(f32[6,2,16,128]{3,2,1,0:T(8,128)S(1)} %copy.174), channel_id=1, source_target_pairs={{32,0},{48,16},{64,32},{80,48},{96,64},{112,80},{128,96},{144,112}... | collective-permute-start | bytes 294920 | tf_op jit(solution)/shard_map/ppermute | solution.py:18
  34.2 3.8 %collective-permute-done.3 = f32[6,2,16,128]{3,2,1,0:T(8,128)S(1)} collective-permute-done((f32[6,2,16,128]{3,2,1,0:T(8,128)S(1)}, f32[6,2,16,128]{3,2,1,0:T(8,128)S(1)}, u32[]{:S(2)}, u32[]{:S(2)}) %collective-permute-start.3) | collective-permute-done | bytes 98336 | tf_op jit(solution)/shard_map/ppermute | solution.py:18
  38.1 5.5 %copy.176 = f32[6,5,2,16,128]{0,4,3,2,1:T(8,128)} copy(f32[6,5,2,16,128]{4,3,1,0,2:T(8,128)S(1)} %bitcast_dynamic-update-slice_fusion) | data formatting | bytes 983040 | tf_op jit(solution)/shard_map/stack | solution.py:93
  43.6 9.4 %gather_fusion.1 = f32[2048,6]{1,0:T(8,128)S(1)} fusion(f32[6,20480]{0,1:T(8,128)} %bitcast.91, s32[2048]{0:T(1024)S(1)} %broadcast_clamp_fusion.1), kind=kCustom, calls=%fused_computation.7 | custom fusion | bytes 106496 | tf_op jit(solution)/shard_map/jit(_take)/gather | solution.py:95
  53.0 0.7 multiply_reduce_fusion
  53.8 0.1 constant_dynamic-update-slice_fusion.2
  53.9 0.7 gather_fusion.3
  54.6 0.1 select_bitcast_fusion.6
  54.7 4.3 %collective-permute-start.4 = (f32[6,256]{0,1:T(8,128)S(1)}, f32[6,256]{0,1:T(8,128)S(1)}, u32[]{:S(2)}, u32[]{:S(2)}) collective-permute-start(f32[6,256]{0,1:T(8,128)S(1)} %select_bitcast_fusion.6), channel_id=1, source_target_pairs={{0,16},{1,17},{2,18},{3,19},{4,20},{5,21},{6,22},{7,23},{8,24},{9,... | collective-permute-start | bytes 18440 | tf_op jit(solution)/shard_map/ppermute | solution.py:18
  59.1 0.7 gather_fusion.4
  59.8 0.1 select_bitcast_fusion.5
  59.9 4.7 %collective-permute-start.5 = (f32[6,256]{0,1:T(8,128)S(1)}, f32[6,256]{0,1:T(8,128)S(1)}, u32[]{:S(2)}, u32[]{:S(2)}) collective-permute-start(f32[6,256]{0,1:T(8,128)S(1)} %select_bitcast_fusion.5), channel_id=1, source_target_pairs={{16,0},{17,1},{18,2},{19,3},{20,4},{21,5},{22,6},{23,7},{24,8},{25... | collective-permute-start | bytes 18440 | tf_op jit(solution)/shard_map/ppermute | solution.py:18
  64.7 0.7 gather_fusion.5
  65.4 0.1 select_bitcast_fusion.4
  65.5 3.5 %collective-permute-start.6 = (f32[6,256]{0,1:T(8,128)S(1)}, f32[6,256]{0,1:T(8,128)S(1)}, u32[]{:S(2)}, u32[]{:S(2)}) collective-permute-start(f32[6,256]{0,1:T(8,128)S(1)} %select_bitcast_fusion.4), channel_id=1, source_target_pairs={{0,2},{1,3},{2,4},{3,5},{4,6},{5,7},{6,8},{7,9},{8,10},{9,11},{10,... | collective-permute-start | bytes 18440 | tf_op jit(solution)/shard_map/ppermute | solution.py:18
  69.0 0.7 gather_fusion.6
  69.7 0.1 select_bitcast_fusion.3
  69.8 6.6 %collective-permute-start.7 = (f32[6,256]{0,1:T(8,128)S(1)}, f32[6,256]{0,1:T(8,128)S(1)}, u32[]{:S(2)}, u32[]{:S(2)}) collective-permute-start(f32[6,256]{0,1:T(8,128)S(1)} %select_bitcast_fusion.3), channel_id=1, source_target_pairs={{2,0},{3,1},{4,2},{5,3},{6,4},{7,5},{8,6},{9,7},{10,8},{11,9},{12,... | collective-permute-start | bytes 18440 | tf_op jit(solution)/shard_map/ppermute | solution.py:18
  76.4 0.7 gather_fusion.7
  77.1 0.1 select_bitcast_fusion.2
  77.2 1.9 collective-permute-start.8
  79.2 0.7 gather_fusion.8
  79.9 0.1 select_bitcast_fusion.1
  80.0 7.9 %collective-permute-start.9 = (f32[6,256]{0,1:T(8,128)S(1)}, f32[6,256]{0,1:T(8,128)S(1)}, u32[]{:S(2)}, u32[]{:S(2)}) collective-permute-start(f32[6,256]{0,1:T(8,128)S(1)} %select_bitcast_fusion.1), channel_id=1, source_target_pairs={{1,0},{2,1},{3,2},{4,3},{5,4},{6,5},{7,6},{8,7},{9,8},{10,9},{11,1... | collective-permute-start | bytes 18440 | tf_op jit(solution)/shard_map/ppermute | solution.py:18
  88.0 2.4 collective-permute-done.9
  90.4 34.3 %gather_fusion.2 = f32[10240,6]{1,0:T(8,128)} fusion(f32[6,2048]{0,1:T(8,128)S(1)} %multiply_dynamic-update-slice_fusion, s32[10240]{0:T(1024)S(1)} %broadcast_clamp_fusion), kind=kCustom, calls=%fused_computation.8 | custom fusion | bytes 532480 | tf_op jit(solution)/shard_map/jit(_take)/gather | solution.py:22
  124.7 5.7 %select_bitcast_fusion = f32[6,4,2560]{0,2,1:T(8,128)S(1)} fusion(f32[4,2560,6]{2,1,0:T(8,128)} %bitcast.92, pred[4,2560]{1,0:T(4,128)(4,1)S(1)} %compare_and_fusion), kind=kLoop, calls=%fused_computation.12 | loop fusion | flops 61440 | bytes 501760 | tf_op jit(solution)/shard_map/jit(_take)/select_n | solution.py:22
  130.4 4.1 %slice_reduce_fusion = (f32[3,2560]{0,1:T(8,128)S(1)}, f32[3,4,2560]{0,2,1:T(8,128)}) fusion(f32[6,4,2560]{0,2,1:T(8,128)S(1)} %select_bitcast_fusion), kind=kLoop, calls=%fused_computation.11 | loop fusion | flops 23040 | bytes 399360 | tf_op jit(solution)/shard_map/reduce_sum | solution.py:27
  134.5 3.3 %copy.177 = f32[3,4,2560]{2,1,0:T(4,128)S(1)} copy(f32[3,4,2560]{0,2,1:T(8,128)} %get-tuple-element.26) | data formatting | bytes 245760 | tf_op jit(solution)/shard_map/slice | solution.py:24
  137.8 0.3 multiply_reduce_fusion.2
  138.2 0.4 copy.180
  138.8 0.1 multiply_subtract_fusion
  138.9 0.1 multiply_reduce_fusion.1
  139.1 0.1 pad_maximum_fusion
  139.2 3.1 %copy.183 = f32[10240,4]{1,0:T(8,128)} copy(f32[10240,4]{0,1:T(4,128)S(1)} %bitcast.96) | data formatting | bytes 327680 | tf_op jit(solution)/shard_map/reshape | solution.py:116
  142.3 55.4 %scatter_custom_fusion = f32[2048,4]{1,0:T(8,128)S(1)} fusion(s32[10240]{0:T(1024)S(1)} %reshape.362, f32[10240,4]{1,0:T(8,128)} %copy.183, f32[]{:T(128)} %constant.36.clone.1), kind=kCustom, calls=%fused_computation.14 | custom fusion | flops 40960 | bytes 33280 | tf_op jit(solution)/shard_map/scatter-add | solution.py:117
  197.7 0.3 copy.184
  198.1 1.9 collective-permute-start.10
  200.0 0.1 bitcast_select_fusion
  200.1 0.7 copy.187
  200.8 3.9 %collective-permute-start.11 = (f32[4,256]{1,0:T(4,128)S(1)}, f32[4,256]{1,0:T(4,128)S(1)}, u32[]{:S(2)}, u32[]{:S(2)}) collective-permute-start(f32[4,256]{1,0:T(4,128)S(1)} %get-tuple-element.36), channel_id=1, source_target_pairs={{0,16},{1,17},{2,18},{3,19},{4,20},{5,21},{6,22},{7,23},{8,24},{9,... | collective-permute-start | bytes 12296 | tf_op jit(solution)/shard_map/ppermute | solution.py:18
  204.8 2.7 %collective-permute-start.12 = (f32[4,256]{1,0:T(4,128)S(1)}, f32[4,256]{1,0:T(4,128)S(1)}, u32[]{:S(2)}, u32[]{:S(2)}) collective-permute-start(f32[4,256]{1,0:T(4,128)S(1)} %get-tuple-element.35), channel_id=1, source_target_pairs={{2,0},{3,1},{4,2},{5,3},{6,4},{7,5},{8,6},{9,7},{10,8},{11,9},{12,... | collective-permute-start | bytes 12296 | tf_op jit(solution)/shard_map/ppermute | solution.py:18
  207.5 3.1 %collective-permute-start.13 = (f32[4,256]{1,0:T(4,128)S(1)}, f32[4,256]{1,0:T(4,128)S(1)}, u32[]{:S(2)}, u32[]{:S(2)}) collective-permute-start(f32[4,256]{1,0:T(4,128)S(1)} %get-tuple-element.34), channel_id=1, source_target_pairs={{0,2},{1,3},{2,4},{3,5},{4,6},{5,7},{6,8},{7,9},{8,10},{9,11},{10,... | collective-permute-start | bytes 12296 | tf_op jit(solution)/shard_map/ppermute | solution.py:18
  210.6 13.2 %collective-permute-start.14 = (f32[4,256]{1,0:T(4,128)S(1)}, f32[4,256]{1,0:T(4,128)S(1)}, u32[]{:S(2)}, u32[]{:S(2)}) collective-permute-start(f32[4,256]{1,0:T(4,128)S(1)} %get-tuple-element.33), channel_id=1, source_target_pairs={{1,0},{2,1},{3,2},{4,3},{5,4},{6,5},{7,6},{8,7},{9,8},{10,9},{11,1... | collective-permute-start | bytes 12296 | tf_op jit(solution)/shard_map/ppermute | solution.py:18
  223.8 1.9 collective-permute-start.15
  225.9 7.1 %collective-permute-done.15 = f32[4,256]{1,0:T(4,128)S(1)} collective-permute-done((f32[4,256]{1,0:T(4,128)S(1)}, f32[4,256]{1,0:T(4,128)S(1)}, u32[]{:S(2)}, u32[]{:S(2)}) %collective-permute-start.15) | collective-permute-done | bytes 4128 | tf_op jit(solution)/shard_map/ppermute | solution.py:18
  233.0 0.3 copy.185
  233.3 8.8 %scatter_custom_fusion.1 = f32[512,4]{1,0:T(8,128)S(1)} fusion(s32[1536]{0:T(1024)S(1)} %reshape.370, f32[1536,4]{1,0:T(8,128)S(1)} %copy.185, f32[]{:T(128)} %constant.36.clone.1), kind=kCustom, calls=%fused_computation.28 | custom fusion | flops 6144 | bytes 8196 | tf_op jit(solution)/shard_map/scatter-add | solution.py:127
  242.1 0.1 copy.186
  242.2 0.6 fusion.11
  (95 shorter events, 1.2 us)
Async XLA Ops:
  0.6 19.4 %copy-start.7 = (f32[3]{0:T(128)S(1)}, f32[3]{0:T(128)}, u32[]{:S(2)}) copy-start(f32[3]{0:T(128)} %constant.94.clone) | copy-start | bytes 40
  0.6 18.3 %copy-start.3 = (s32[1,1,1,4,512]{4,3,2,1,0:T(4,128)S(1)}, s32[1,1,1,4,512]{4,3,2,1,0:T(4,128)}, u32[]{:S(2)}) copy-start(s32[1,1,1,4,512]{4,3,2,1,0:T(4,128)} %param.14) | copy-start | bytes 24580
  0.7 18.4 %copy-start.4 = (s32[1,1,1,6,256]{4,2,3,1,0:T(1,128)S(1)}, s32[1,1,1,6,256]{4,2,3,1,0:T(1,128)}, u32[]{:S(2)}) copy-start(s32[1,1,1,6,256]{4,2,3,1,0:T(1,128)} %param.17) | copy-start | bytes 18436
  0.7 18.5 %copy-start = (s32[1,1,1,4,2560]{4,3,2,1,0:T(4,128)S(1)}, s32[1,1,1,4,2560]{4,3,2,1,0:T(4,128)}, u32[]{:S(2)}) copy-start(s32[1,1,1,4,2560]{4,3,2,1,0:T(4,128)} %param.18) | copy-start | bytes 122884
  0.7 18.7 %copy-start.6 = (s32[1,1,1,512]{3,2,1,0:T(1,128)S(1)}, s32[1,1,1,512]{3,2,1,0:T(1,128)}, u32[]{:S(2)}) copy-start(s32[1,1,1,512]{3,2,1,0:T(1,128)} %param.16) | copy-start | bytes 6148
  0.7 18.7 %copy-start.1 = (f32[1,1,1,12,2560]{4,2,3,1,0:T(1,128)S(1)}, f32[1,1,1,12,2560]{4,2,3,1,0:T(1,128)}, u32[]{:S(2)}) copy-start(f32[1,1,1,12,2560]{4,2,3,1,0:T(1,128)} %param.19) | copy-start | bytes 368644
  0.7 19.2 %copy-start.2 = (f32[1,1,1,2560]{3,2,1,0:T(1,128)S(1)}, f32[1,1,1,2560]{3,2,1,0:T(1,128)}, u32[]{:S(2)}) copy-start(f32[1,1,1,2560]{3,2,1,0:T(1,128)} %param.20) | copy-start | bytes 30724
  8.6 14.4 %collective-permute-start = (f32[6,2,16,128]{3,2,1,0:T(8,128)S(1)}, f32[6,2,16,128]{3,2,1,0:T(8,128)S(1)}, u32[]{:S(2)}, u32[]{:S(2)}) collective-permute-start(f32[6,2,16,128]{3,2,1,0:T(8,128)S(1)} %copy.168), channel_id=1, source_target_pairs={{0,32},{16,48},{32,64},{48,80},{64,96},{80,112},{96,128},{112,144}... | collective-permute-start | bytes 294920 | tf_op jit(solution)/shard_map/ppermute | solution.py:18
  14.7 12.4 %collective-permute-start.1 = (f32[6,2,16,128]{3,2,1,0:T(8,128)S(1)}, f32[6,2,16,128]{3,2,1,0:T(8,128)S(1)}, u32[]{:S(2)}, u32[]{:S(2)}) collective-permute-start(f32[6,2,16,128]{3,2,1,0:T(8,128)S(1)} %copy.170), channel_id=1, source_target_pairs={{0,16},{16,32},{32,48},{48,64},{64,80},{80,96},{96,112},{112,128},... | collective-permute-start | bytes 294920 | tf_op jit(solution)/shard_map/ppermute | solution.py:18
  27.1 7.1 %collective-permute-start.2 = (f32[6,2,16,128]{3,2,1,0:T(8,128)S(1)}, f32[6,2,16,128]{3,2,1,0:T(8,128)S(1)}, u32[]{:S(2)}, u32[]{:S(2)}) collective-permute-start(f32[6,2,16,128]{3,2,1,0:T(8,128)S(1)} %copy.172), channel_id=1, source_target_pairs={{16,0},{32,16},{48,32},{64,48},{80,64},{96,80},{112,96},{128,112},... | collective-permute-start | bytes 294920 | tf_op jit(solution)/shard_map/ppermute | solution.py:18
  30.6 7.5 %collective-permute-start.3 = (f32[6,2,16,128]{3,2,1,0:T(8,128)S(1)}, f32[6,2,16,128]{3,2,1,0:T(8,128)S(1)}, u32[]{:S(2)}, u32[]{:S(2)}) collective-permute-start(f32[6,2,16,128]{3,2,1,0:T(8,128)S(1)} %copy.174), channel_id=1, source_target_pairs={{32,0},{48,16},{64,32},{80,48},{96,64},{112,80},{128,96},{144,112}... | collective-permute-start | bytes 294920 | tf_op jit(solution)/shard_map/ppermute | solution.py:18
  38.1 14.9 %copy-start.5 = (f32[1,1,1,4,512]{4,3,2,1,0:T(4,128)S(1)}, f32[1,1,1,4,512]{4,3,2,1,0:T(4,128)}, u32[]{:S(2)}) copy-start(f32[1,1,1,4,512]{4,3,2,1,0:T(4,128)} %param.15) | copy-start | bytes 24580
  54.7 25.3 %collective-permute-start.4 = (f32[6,256]{0,1:T(8,128)S(1)}, f32[6,256]{0,1:T(8,128)S(1)}, u32[]{:S(2)}, u32[]{:S(2)}) collective-permute-start(f32[6,256]{0,1:T(8,128)S(1)} %select_bitcast_fusion.6), channel_id=1, source_target_pairs={{0,16},{1,17},{2,18},{3,19},{4,20},{5,21},{6,22},{7,23},{8,24},{9,... | collective-permute-start | bytes 18440 | tf_op jit(solution)/shard_map/ppermute | solution.py:18
  59.9 28.0 %collective-permute-start.5 = (f32[6,256]{0,1:T(8,128)S(1)}, f32[6,256]{0,1:T(8,128)S(1)}, u32[]{:S(2)}, u32[]{:S(2)}) collective-permute-start(f32[6,256]{0,1:T(8,128)S(1)} %select_bitcast_fusion.5), channel_id=1, source_target_pairs={{16,0},{17,1},{18,2},{19,3},{20,4},{21,5},{22,6},{23,7},{24,8},{25... | collective-permute-start | bytes 18440 | tf_op jit(solution)/shard_map/ppermute | solution.py:18
  65.5 22.4 %collective-permute-start.6 = (f32[6,256]{0,1:T(8,128)S(1)}, f32[6,256]{0,1:T(8,128)S(1)}, u32[]{:S(2)}, u32[]{:S(2)}) collective-permute-start(f32[6,256]{0,1:T(8,128)S(1)} %select_bitcast_fusion.4), channel_id=1, source_target_pairs={{0,2},{1,3},{2,4},{3,5},{4,6},{5,7},{6,8},{7,9},{8,10},{9,11},{10,... | collective-permute-start | bytes 18440 | tf_op jit(solution)/shard_map/ppermute | solution.py:18
  69.8 18.2 %collective-permute-start.7 = (f32[6,256]{0,1:T(8,128)S(1)}, f32[6,256]{0,1:T(8,128)S(1)}, u32[]{:S(2)}, u32[]{:S(2)}) collective-permute-start(f32[6,256]{0,1:T(8,128)S(1)} %select_bitcast_fusion.3), channel_id=1, source_target_pairs={{2,0},{3,1},{4,2},{5,3},{6,4},{7,5},{8,6},{9,7},{10,8},{11,9},{12,... | collective-permute-start | bytes 18440 | tf_op jit(solution)/shard_map/ppermute | solution.py:18
  77.2 10.8 %collective-permute-start.8 = (f32[6,256]{0,1:T(8,128)S(1)}, f32[6,256]{0,1:T(8,128)S(1)}, u32[]{:S(2)}, u32[]{:S(2)}) collective-permute-start(f32[6,256]{0,1:T(8,128)S(1)} %select_bitcast_fusion.2), channel_id=1, source_target_pairs={{0,1},{1,2},{2,3},{3,4},{4,5},{5,6},{6,7},{7,8},{8,9},{9,10},{10,1... | collective-permute-start | bytes 18440 | tf_op jit(solution)/shard_map/ppermute | solution.py:18
  80.0 10.4 %collective-permute-start.9 = (f32[6,256]{0,1:T(8,128)S(1)}, f32[6,256]{0,1:T(8,128)S(1)}, u32[]{:S(2)}, u32[]{:S(2)}) collective-permute-start(f32[6,256]{0,1:T(8,128)S(1)} %select_bitcast_fusion.1), channel_id=1, source_target_pairs={{1,0},{2,1},{3,2},{4,3},{5,4},{6,5},{7,6},{8,7},{9,8},{10,9},{11,1... | collective-permute-start | bytes 18440 | tf_op jit(solution)/shard_map/ppermute | solution.py:18
  198.1 25.8 %collective-permute-start.10 = (f32[4,256]{1,0:T(4,128)S(1)}, f32[4,256]{1,0:T(4,128)S(1)}, u32[]{:S(2)}, u32[]{:S(2)}) collective-permute-start(f32[4,256]{1,0:T(4,128)S(1)} %get-tuple-element.37), channel_id=1, source_target_pairs={{16,0},{17,1},{18,2},{19,3},{20,4},{21,5},{22,6},{23,7},{24,8},{25... | collective-permute-start | bytes 12296 | tf_op jit(solution)/shard_map/ppermute | solution.py:18
  200.8 24.9 %collective-permute-start.11 = (f32[4,256]{1,0:T(4,128)S(1)}, f32[4,256]{1,0:T(4,128)S(1)}, u32[]{:S(2)}, u32[]{:S(2)}) collective-permute-start(f32[4,256]{1,0:T(4,128)S(1)} %get-tuple-element.36), channel_id=1, source_target_pairs={{0,16},{1,17},{2,18},{3,19},{4,20},{5,21},{6,22},{7,23},{8,24},{9,... | collective-permute-start | bytes 12296 | tf_op jit(solution)/shard_map/ppermute | solution.py:18
  204.8 21.0 %collective-permute-start.12 = (f32[4,256]{1,0:T(4,128)S(1)}, f32[4,256]{1,0:T(4,128)S(1)}, u32[]{:S(2)}, u32[]{:S(2)}) collective-permute-start(f32[4,256]{1,0:T(4,128)S(1)} %get-tuple-element.35), channel_id=1, source_target_pairs={{2,0},{3,1},{4,2},{5,3},{6,4},{7,5},{8,6},{9,7},{10,8},{11,9},{12,... | collective-permute-start | bytes 12296 | tf_op jit(solution)/shard_map/ppermute | solution.py:18
  207.5 18.3 %collective-permute-start.13 = (f32[4,256]{1,0:T(4,128)S(1)}, f32[4,256]{1,0:T(4,128)S(1)}, u32[]{:S(2)}, u32[]{:S(2)}) collective-permute-start(f32[4,256]{1,0:T(4,128)S(1)} %get-tuple-element.34), channel_id=1, source_target_pairs={{0,2},{1,3},{2,4},{3,5},{4,6},{5,7},{6,8},{7,9},{8,10},{9,11},{10,... | collective-permute-start | bytes 12296 | tf_op jit(solution)/shard_map/ppermute | solution.py:18
  210.6 15.2 %collective-permute-start.14 = (f32[4,256]{1,0:T(4,128)S(1)}, f32[4,256]{1,0:T(4,128)S(1)}, u32[]{:S(2)}, u32[]{:S(2)}) collective-permute-start(f32[4,256]{1,0:T(4,128)S(1)} %get-tuple-element.33), channel_id=1, source_target_pairs={{1,0},{2,1},{3,2},{4,3},{5,4},{6,5},{7,6},{8,7},{9,8},{10,9},{11,1... | collective-permute-start | bytes 12296 | tf_op jit(solution)/shard_map/ppermute | solution.py:18
  223.8 9.1 %collective-permute-start.15 = (f32[4,256]{1,0:T(4,128)S(1)}, f32[4,256]{1,0:T(4,128)S(1)}, u32[]{:S(2)}, u32[]{:S(2)}) collective-permute-start(f32[4,256]{1,0:T(4,128)S(1)} %get-tuple-element.32), channel_id=1, source_target_pairs={{0,1},{1,2},{2,3},{3,4},{4,5},{5,6},{6,7},{7,8},{8,9},{9,10},{10,1... | collective-permute-start | bytes 12296 | tf_op jit(solution)/shard_map/ppermute | solution.py:18
where the time goes:
time: 244 us; the launch traced here: 243 us
  other arithmetic  79.3 us (32%)
  starting transfers between devices  73.1 us (30%)
  local copies, waits for them, and re-layouts  64.4 us (26%)
  waiting for transfers between devices  20.3 us (8%)
  blocking collectives  4.11 us (2%)
    ppermute x16, starting transfers between devices, passed_along(): lax.ppermute(value, axis, [(source, source + steps) for source in range(f...  73.1 us
    scatter-add x1, other arithmetic, per_device(): jax.ops.segment_sum(flat_terms, nodes.reshape(-1), num_segments=width)  55.4 us
    gather x1, local copies, waits for them, and re-layouts, element_residual(): values = jnp.take(node_table, elem_nodes, axis=1)  34.3 us
    ppermute x16, waiting for transfers between devices, passed_along(): lax.ppermute(value, axis, [(source, source + steps) for source in range(f...  20.3 us
    gather x1, local copies, waits for them, and re-layouts, per_device(): gathered = jnp.take(received, node_slots[0, 0, 0], axis=1)  9.44 us
    scatter-add x1, other arithmetic, per_device(): jax.ops.segment_sum(all_returned.T, halos.reshape(-1), num_segments=owned)  8.81 us
    select_n x2, other arithmetic, element_residual(): values = jnp.take(node_table, elem_nodes, axis=1)  5.76 us
    another operation x2, local copies, waits for them, and re-layouts, per_device(): received = jnp.stack(columns, axis=1)  5.49 us
  transfers between devices with their start and end apart: 16, of which 5 were waited for; matrix products, arithmetic and copies ran while one was open for 2% of the time, Pallas kernels for 0%

commit v1 on v0

v1 whole, which is shorter than its diff:
```python
import functools

import jax
import jax.numpy as jnp
from jax import lax
from jax.experimental import pallas as pl
from jax.experimental.pallas import tpu as pltpu
from jax.sharding import PartitionSpec as P

MESH = pl.DeviceIdType.MESH
F32 = jnp.float32
BF16 = jnp.bfloat16
LANES = 128
FIELDS = 6
ROWS = 4
SIDES = 5
SPOTS = 80
CAP = 16

ocean_temp = 0.0
strain_reg = 0.01
gravity = 0.5


def lane_gather(row, lanes):
    return jnp.take_along_axis(row, lanes, axis=1)


def split_two(value):
    high = value.astype(BF16).astype(F32)
    return high, value - high


def kernel(
    count_x,
    count_y,
    blocks,
    old,
    slots,
    weights,
    front,
    halos,
    nodes,
    grads,
    volume,
    out_new,
    out_res,
    req_slots,
    req_weights,
    part_out,
    part_in,
    state,
    pairs,
    halo_idx,
    halo_out,
    ghost_in,
    spot_idx,
    values,
    vol_rows,
    contrib,
    left,
    right,
    ret_out,
    ret_in,
    own_sum,
    req_send,
    req_recv,
    part_send,
    part_recv,
    halo_send,
    halo_recv,
    ret_send,
    ret_recv,
):
    x = lax.axis_index("mapx")
    y = lax.axis_index("mapy")
    layer = lax.axis_index("layer")

    def device(dx, dy, which):
        return (lax.rem(x + dx + count_x, count_x), lax.rem(y + dy + count_y, count_y), which)

    far = [(t, lp) for t in (-2, 2, -1, 1) for lp in (0, 1)]
    peers = [((t + 2) * 2 + lp, (2 - t) * 2 + layer, device(t, 0, lp)) for t, lp in far]
    peers.append((4 + (1 - layer), 4 + layer, device(0, 0, 1 - layer)))
    sides = [device(1, 0, layer), device(-1, 0, layer), device(0, 1, layer), device(0, -1, layer), device(0, 0, 1 - layer)]
    backs = [sides[1], sides[0], sides[3], sides[2], sides[4]]

    barrier = pltpu.get_barrier_semaphore()
    greet = [peer[2] for peer in peers] + [sides[2], sides[3]]
    for other in greet:
        pl.semaphore_signal(barrier, inc=1, device_id=other, device_id_type=MESH)

    me = 4 + layer
    for j in range(ROWS):
        req_slots[10, pl.ds(j, 4, stride=4), :] = slots[:, j * LANES : (j + 1) * LANES]
        req_weights[10, pl.ds(j, 4, stride=4), :] = weights[:, j * LANES : (j + 1) * LANES]
    pl.semaphore_wait(barrier, len(greet))

    def request(number, theirs, other):
        return [
            pltpu.make_async_remote_copy(
                src_ref=ref.at[10],
                dst_ref=ref.at[theirs],
                send_sem=req_send.at[which, number],
                recv_sem=req_recv.at[which, theirs],
                device_id=other,
                device_id_type=MESH,
            )
            for which, ref in enumerate((req_slots, req_weights))
        ]

    def request_in(number, other):
        for which, ref in enumerate((req_slots, req_weights)):
            pltpu.make_async_remote_copy(
                src_ref=ref.at[10],
                dst_ref=ref.at[number],
                send_sem=req_send.at[which, number],
                recv_sem=req_recv.at[which, number],
                device_id=other,
                device_id_type=MESH,
            ).wait_recv()

    for peer in peers:
        for copy in request(*peer):
            copy.start()

    def partial(spot, number, theirs, dest):
        lo, blk, wgt = [], [], []
        for v in range(2):
            s = req_slots[spot, v * 8 : (v + 1) * 8, :]
            lo.append(jnp.bitwise_and(s, LANES - 1))
            blk.append(jnp.right_shift(s, 7) - theirs * CAP)
            wgt.append(req_weights[spot, v * 8 : (v + 1) * 8, :])

        def step(c, acc):
            b = blocks[number, c]
            hit = [blk[v] == c for v in range(2)]
            new = []
            for f in range(FIELDS):
                row = jnp.broadcast_to(old[f, pl.ds(b, 1), :], (8, LANES))
                for v in range(2):
                    new.append(jnp.where(hit[v], lane_gather(row, lo[v]), acc[f * 2 + v]))
            return tuple(new)

        acc = lax.fori_loop(0, CAP, step, tuple(jnp.zeros((8, LANES), F32) for _ in range(12)), unroll=2)
        for f in range(FIELDS):
            both = acc[f * 2] * wgt[0] + acc[f * 2 + 1] * wgt[1]
            part_out[dest, f * 4 : (f + 1) * 4, :] = both[0:4] + both[4:8]

    def send_part(number, theirs, other):
        return pltpu.make_async_remote_copy(
            src_ref=part_out.at[number],
            dst_ref=part_in.at[theirs],
            send_sem=part_send.at[number],
            recv_sem=part_recv.at[theirs],
            device_id=other,
            device_id_type=MESH,
        )

    partial(10, me, me, 10)

    for j in range(20):
        spot_idx[j * 4 : (j + 1) * 4, :] = nodes[:, j * LANES : (j + 1) * LANES]
    for j in range(5):
        vol_rows[j * 4 : (j + 1) * 4, :] = volume[j]
    for k in range(SIDES):
        pair = halos[k] if k < 4 else halos[4 + layer]
        for d in range(4):
            halo_idx[k, d * 2 : (d + 1) * 2, :] = pair

    for number, theirs, other in [peers[8]] + peers[:8]:
        request_in(number, other)
        partial(number, number, theirs, number)
        send_part(number, theirs, other).start()

    total = part_out[10]
    for number, theirs, other in [peers[8]] + peers[:8]:
        pltpu.make_async_remote_copy(
            src_ref=part_out.at[number],
            dst_ref=part_in.at[number],
            send_sem=part_send.at[number],
            recv_sem=part_recv.at[number],
            device_id=other,
            device_id_type=MESH,
        ).wait_recv()
        total = total + part_in[number]
    state[...] = total
    state[16:20, :] = jnp.where(front[...] == 1, ocean_temp, state[16:20, :])

    for h in range(ROWS):
        for f in range(8):
            src = f if f < FIELDS else f - 2
            pairs[h, f * 2 : (f + 1) * 2, :] = jnp.broadcast_to(state[pl.ds(src * 4 + h, 1), :], (2, LANES))

    def halo_copy(k):
        return pltpu.make_async_remote_copy(
            src_ref=halo_out.at[k],
            dst_ref=ghost_in.at[k],
            send_sem=halo_send.at[k],
            recv_sem=halo_recv.at[k],
            device_id=sides[k],
            device_id_type=MESH,
        )

    for k in range(SIDES):
        idx = halo_idx[k]
        lo = jnp.bitwise_and(idx, LANES - 1)
        hi = jnp.right_shift(idx, 7)
        for g in range(2):
            acc = jnp.zeros((8, LANES), F32)
            for h in range(ROWS):
                acc = jnp.where(hi == h, lane_gather(pairs[h, g * 8 : (g + 1) * 8, :], lo), acc)
            halo_out[k, g * 8 : (g + 1) * 8, :] = acc
        halo_copy(k).start()

    for f in range(FIELDS):
        out_new[f] = state[f * 4 : (f + 1) * 4, :]

    def gather_rows(t, table, first):
        at = pl.ds(pl.multiple_of(t * 8, 8), 8)
        idx = spot_idx[at, :]
        lo = jnp.bitwise_and(idx, LANES - 1)
        hi = jnp.right_shift(idx, 7)
        acc = [jnp.zeros((8, LANES), F32) if first else values[f, at, :] for f in range(FIELDS)]
        for code, fetch in table:
            hit = hi == code
            for f in range(FIELDS):
                row = jnp.broadcast_to(fetch(f), (8, LANES))
                acc[f] = jnp.where(hit, lane_gather(row, lo), acc[f])
        for f in range(FIELDS):
            values[f, at, :] = acc[f]

    own_table = [(h, lambda f, h=h: state[f * 4 + h : f * 4 + h + 1, :]) for h in range(ROWS)]
    lax.fori_loop(0, SPOTS // 8, lambda t, c: (gather_rows(t, own_table, True), c)[1], 0)

    low_x, high_x = x > 0, x < count_x - 1
    low_y, high_y = y > 0, y < count_y - 1
    ghost_live = [low_x, high_x, low_y, high_y]
    back_live = [high_x, low_x, high_y, low_y]
    ghost_table = []
    for k in range(SIDES):
        for r in range(2):
            code = jnp.where(ghost_live[k], 4 + 2 * k + r, -1) if k < 4 else 4 + 2 * (5 - layer) + r
            ghost_table.append((code, lambda f, k=k, r=r: ghost_in[k, f * 2 + r : f * 2 + r + 1, :]))
    for k in range(SIDES):
        halo_copy(k).wait_recv()
    lax.fori_loop(0, SPOTS // 8, lambda t, c: (gather_rows(t, ghost_table, False), c)[1], 0)

    for r0 in (0, 8, 12):
        val = [[values[f, pl.ds(r0 * 4 + a, 8, stride=4), :] for a in range(4)] for f in range(FIELDS)]
        grad = [[grads[(3 * a + j) * 20 + r0 : (3 * a + j) * 20 + r0 + 8, :] for j in range(3)] for a in range(4)]
        vol = vol_rows[r0 : r0 + 8, :]
        vg = [[sum(val[i][a] * grad[a][j] for a in range(4)) for j in range(3)] for i in range(3)]
        strain = [[0.5 * (vg[i][j] + vg[j][i]) for j in range(3)] for i in range(3)]
        second = 0.5 * sum(strain[i][j] * strain[i][j] for i in range(3) for j in range(3))
        pm, tm, dm = [0.25 * (val[f][0] + val[f][1] + val[f][2] + val[f][3]) for f in (3, 4, 5)]
        visc2 = (1.0 - dm) * jnp.exp(-tm) * jnp.exp(jnp.log(second + strain_reg) * (-1.0 / 3.0))
        stress = [[visc2 * strain[i][j] - (pm if i == j else 0.0) for j in range(3)] for i in range(3)]
        cont = 0.25 * vol * (vg[0][0] + vg[1][1] + vg[2][2])
        for a in range(4):
            for c in range(4):
                if c < 3:
                    part = vol * sum(stress[c][j] * grad[a][j] for j in range(3))
                    if c == 2:
                        part = part + 0.25 * gravity * vol
                else:
                    part = cont
                for d in range(2):
                    contrib[pl.ds((r0 * 4 + a) * 8 + d * 4 + c, 8, stride=32), :] = part

    sub = lax.broadcasted_iota(jnp.int32, (8, LANES), 0)
    half = jnp.right_shift(sub, 2)

    def one_hot(lo_row, u):
        cols = []
        for g in range(16):
            cols.append(jnp.where(lo_row == sub + g * 8, 1.0, 0.0))
        right[:, u * LANES : (u + 1) * LANES] = jnp.concatenate(cols, axis=0).astype(BF16)

    def chunk(t, acc):
        for u in range(8):
            s = t * 8 + u
            idx = jnp.broadcast_to(spot_idx[pl.ds(s, 1), :], (8, LANES))
            one_hot(jnp.bitwise_and(idx, LANES - 1), u)
            hi = jnp.right_shift(idx, 7) - half
            parts = split_two(contrib[pl.ds(pl.multiple_of(s * 8, 8), 8), :])
            for part in range(2):
                rows = [jnp.where(hi == 2 * m, parts[part], 0.0) for m in range(8)]
                left[part * 64 : (part + 1) * 64, u * LANES : (u + 1) * LANES] = jnp.concatenate(rows, axis=0).astype(BF16)
        return acc + lax.dot_general(left[...], right[...], (((1,), (1,)), ((), ())), preferred_element_type=F32)

    acc = lax.fori_loop(0, SPOTS // 8, chunk, jnp.zeros((128, LANES), F32))
    sums = acc[0:64] + acc[64:128]
    own_sum[...] = sums

    def ret_copy(k):
        return pltpu.make_async_remote_copy(
            src_ref=ret_out.at[k],
            dst_ref=ret_in.at[k],
            send_sem=ret_send.at[k],
            recv_sem=ret_recv.at[k],
            device_id=backs[k],
            device_id_type=MESH,
        )

    for k in range(4):
        ret_out[k] = own_sum[16 + k * 8 : 24 + k * 8, :]
    ret_out[4] = own_sum[pl.ds(pl.multiple_of(16 + (5 - layer) * 8, 8), 8), :]
    for k in range(SIDES):
        ret_copy(k).start()

    final = jnp.zeros((32, LANES), F32)
    for k in range(SIDES):
        for r in range(2):
            u = k * 2 + r
            idx = jnp.broadcast_to(halo_idx[k, r : r + 1, :], (8, LANES))
            one_hot(jnp.bitwise_and(idx, LANES - 1), u % 8) if u < 8 else None
    for k in range(SIDES):
        ret_copy(k).wait_recv()

    def returned(k, r, u):
        idx = jnp.broadcast_to(halo_idx[k, r : r + 1, :], (8, LANES))
        hi = jnp.right_shift(idx, 7) - half
        four = ret_in[k, r * 4 : (r + 1) * 4, :]
        value = jnp.concatenate([four, four], axis=0)
        if k < 4:
            value = jnp.where(back_live[k], value, 0.0)
        parts = split_two(value)
        for part in range(2):
            rows = [jnp.where(hi == 2 * m, parts[part], 0.0) for m in range(2)]
            left[part * 16 : (part + 1) * 16, u * LANES : (u + 1) * LANES] = jnp.concatenate(rows, axis=0).astype(BF16)

    for u in range(8):
        returned(u // 2, u % 2, u)
    final = lax.dot_general(left[0:32, :], right[...], (((1,), (1,)), ((), ())), preferred_element_type=F32)
    for r in range(2):
        idx = jnp.broadcast_to(halo_idx[4, r : r + 1, :], (8, LANES))
        one_hot(jnp.bitwise_and(idx, LANES - 1), r)
        returned(4, r, r)
    final = final + lax.dot_general(
        left[0:32, 0:256], right[:, 0:256], (((1,), (1,)), ((), ())), preferred_element_type=F32
    )
    result = own_sum[0:16, :] + final[0:16] + final[16:32]
    for h in range(ROWS):
        out_res[:, h * LANES : (h + 1) * LANES] = result[h * 4 : (h + 1) * 4]

    for peer in peers:
        for copy in request(*peer):
            copy.wait_send()
        send_part(*peer).wait_send()
    for k in range(SIDES):
        halo_copy(k).wait_send()
        ret_copy(k).wait_send()


def per_device(old_state, send_blocks, node_slots, node_weights, front_mask, halo_lists, elem_nodes, shape_grads, elem_volume):
    count_x = lax.axis_size("mapx")
    count_y = lax.axis_size("mapy")
    vmem = pl.BlockSpec(memory_space=pltpu.VMEM)
    smem = pl.BlockSpec(memory_space=pltpu.SMEM)
    dma = pltpu.SemaphoreType.DMA
    new_state, residual = pl.pallas_call(
        functools.partial(kernel, count_x, count_y),
        out_shape=(
            jax.ShapeDtypeStruct((FIELDS, ROWS, LANES), F32),
            jax.ShapeDtypeStruct((4, ROWS * LANES), F32),
        ),
        in_specs=[smem] + [vmem] * 8,
        out_specs=(vmem, vmem),
        scratch_shapes=[
            pltpu.VMEM((11, 16, LANES), jnp.int32),
            pltpu.VMEM((11, 16, LANES), F32),
            pltpu.VMEM((11, 24, LANES), F32),
            pltpu.VMEM((10, 24, LANES), F32),
            pltpu.VMEM((24, LANES), F32),
            pltpu.VMEM((4, 16, LANES), F32),
            pltpu.VMEM((SIDES, 8, LANES), jnp.int32),
            pltpu.VMEM((SIDES, 16, LANES), F32),
            pltpu.VMEM((SIDES, 16, LANES), F32),
            pltpu.VMEM((SPOTS, LANES), jnp.int32),
            pltpu.VMEM((FIELDS, SPOTS, LANES), F32),
            pltpu.VMEM((24, LANES), F32),
            pltpu.VMEM((SPOTS * 8, LANES), F32),
            pltpu.VMEM((128, 1024), BF16),
            pltpu.VMEM((128, 1024), BF16),
            pltpu.VMEM((SIDES, 8, LANES), F32),
            pltpu.VMEM((SIDES, 8, LANES), F32),
            pltpu.VMEM((64, LANES), F32),
            dma((2, 10)),
            dma((2, 10)),
            dma((10,)),
            dma((10,)),
            dma((SIDES,)),
            dma((SIDES,)),
            dma((SIDES,)),
            dma((SIDES,)),
        ],
        compiler_params=pltpu.CompilerParams(collective_id=0, has_side_effects=True),
        name="remap_residual",
    )(
        send_blocks.reshape(10, CAP),
        old_state.reshape(FIELDS, 64, LANES),
        node_slots.reshape(4, 512),
        node_weights.reshape(4, 512),
        front_mask.reshape(ROWS, LANES),
        halo_lists.reshape(6, 2, LANES),
        elem_nodes.reshape(4, 2560),
        shape_grads.reshape(240, LANES),
        elem_volume.reshape(5, 4, LANES),
    )
    return new_state.reshape(1, 1, 1, FIELDS, 512), residual.reshape(1, 1, 1, 4, 512)


def solution(mesh):
    deep = P("mapx", "mapy", "layer", None, None)
    flat = P("mapx", "mapy", "layer", None)
    return jax.shard_map(
        per_device,
        mesh=mesh,
        in_specs=(deep, deep, deep, deep, flat, deep, deep, deep, flat),
        out_specs=(deep, deep),
        check_vma=False,
    )
```

time: 244 us -> 46.2 us (0.19)
  the two profiles are of different devices: /device:TPU:6 before, /device:TPU:1 now
where the time goes in v1:
time: 46.2 us; the launch traced here: 46 us
  Pallas kernels  42.1 us (91%)
  local copies, waits for them, and re-layouts  3.2 us (7%)
  between operations  0.66 us (1%)
    pallas_call x1, Pallas kernels, per_device(): pl.pallas_call(functools.partial(kernel, count_x, count_y), out_shape=(ja...  42.1 us
    unnamed x7, local copies, waits for them, and re-layouts  3.2 us

profile of v1, /device:TPU:1, one launch (start us, length us, event | category | flops | bytes accessed | tf_op | source)
XLA Modules:
  0.0 46.0 jit_solution(10014204504262590752)
XLA Ops:
  0.6 0.0 copy-start.1
  0.6 0.7 %copy-done.1 = s32[1,1,1,10,16]{4,2,3,1,0:T(1,128)S(1)} copy-done((s32[1,1,1,10,16]{4,2,3,1,0:T(1,128)S(1)}, s32[1,1,1,10,16]{4,2,3,1,0:T(1,128)}, u32[]{:S(2)}) %copy-start.1) | copy-done | bytes 664
  1.3 0.6 %copy.15 = s32[1,1,1,10,16]{4,3,2,1,0:T(8,128)} copy(s32[1,1,1,10,16]{4,2,3,1,0:T(1,128)S(1)} %copy-done.1) | data formatting | bytes 1280
  1.9 42.1 %remap_residual.1 = (f32[6,4,128]{2,1,0:T(4,128)}, f32[4,512]{1,0:T(4,128)}) custom-call(s32[10,16]{1,0:T(8,128)} %bitcast.16, f32[6,64,128]{2,1,0:T(8,128)} %bitcast.13, s32[4,512]{1,0:T(4,128)} %bitcast.19, f32[4,512]{1,0:T(4,128)} %bitcast.20, s32[4,128]{1,0:T(4,128)} %bitcast.23, s32[6,2,128]{2,1,0:T(2,128)} %bitcast.22, s32[4,2560]{1,0:T(4,128)} %bitcast.15, ...), custom_call_target="tpu_custom_call" | custom-call | tf_op jit(solution)/shard_map/remap_residual/pallas_call | solution.py:362
  44.1 0.0 copy-start
  44.1 1.3 %copy.18 = f32[1,1,1,6,512]{4,2,3,1,0:T(1,128)} copy(f32[1,1,1,6,512]{4,2,3,1,0:T(1,128)} %bitcast.17) | data formatting | bytes 24576
  45.4 0.0 copy-done
  45.4 0.6 %copy.19 = f32[1,1,1,4,512]{4,3,2,1,0:T(4,128)} copy(f32[1,1,1,4,512]{4,3,2,1,0:T(4,128)S(1)} %bitcast.21) | data formatting | bytes 16384
Async XLA Ops:
  0.6 0.7 %copy-start.1 = (s32[1,1,1,10,16]{4,2,3,1,0:T(1,128)S(1)}, s32[1,1,1,10,16]{4,2,3,1,0:T(1,128)}, u32[]{:S(2)}) copy-start(s32[1,1,1,10,16]{4,2,3,1,0:T(1,128)} %param.10) | copy-start | bytes 1924
  44.1 1.3 %copy-start = (f32[4,512]{1,0:T(4,128)S(1)}, f32[4,512]{1,0:T(4,128)}, u32[]{:S(2)}) copy-start(f32[4,512]{1,0:T(4,128)} %get-tuple-element.5) | copy-start | bytes 24580

commit v2 on v1

v2 whole, which is shorter than its diff:
```python
import functools

import jax
import jax.numpy as jnp
from jax import lax
from jax.experimental import pallas as pl
from jax.experimental.pallas import tpu as pltpu
from jax.sharding import PartitionSpec as P

MESH = pl.DeviceIdType.MESH
F32 = jnp.float32
BF16 = jnp.bfloat16
LANES = 128
WIDE = 256
FIELDS = 6
ROWS = 4
SIDES = 5
SPOTS = 80
CAP = 16

ocean_temp = 0.0
strain_reg = 0.01
gravity = 0.5


def lane_gather(row, lanes):
    return jnp.take_along_axis(row, lanes, axis=1)


def split_two(value):
    high = value.astype(BF16).astype(F32)
    return high, value - high


def lane_tile(s):
    return pl.ds(pl.multiple_of(s * LANES, LANES), LANES)


def kernel(
    count_x,
    count_y,
    blocks_in,
    old_in,
    slots_in,
    weights_in,
    front_in,
    halos_in,
    nodes_in,
    grads_in,
    volume_in,
    out,
    blocks,
    old,
    slots,
    weights,
    front,
    halos,
    nodes,
    grads,
    volume,
    block_out,
    block_in,
    lookup,
    weight_rows,
    state,
    halo_idx,
    halo_out,
    ghost_in,
    spot_idx,
    one_hot,
    halo_hot,
    values,
    vol_rows,
    contrib,
    left,
    left_back,
    sums,
    ret_out,
    ret_in,
    in_sem,
    block_send,
    block_recv,
    halo_send,
    halo_recv,
    ret_send,
    ret_recv,
):
    x = lax.axis_index("mapx")
    y = lax.axis_index("mapy")
    layer = lax.axis_index("layer")

    def device(dx, dy, which):
        return (lax.rem(x + dx + count_x, count_x), lax.rem(y + dy + count_y, count_y), which)

    far = [(t, lp) for t in (-2, 2, -1, 1) for lp in (0, 1)]
    peers = [((t + 2) * 2 + lp, (2 - t) * 2 + layer, device(t, 0, lp)) for t, lp in far]
    peers.append((4 + (1 - layer), 4 + layer, device(0, 0, 1 - layer)))
    sides = [device(1, 0, layer), device(-1, 0, layer), device(0, 1, layer), device(0, -1, layer), device(0, 0, 1 - layer)]
    backs = [sides[1], sides[0], sides[3], sides[2], sides[4]]

    barrier = pltpu.get_barrier_semaphore()
    greet = [peer[2] for peer in peers] + [sides[2], sides[3]]
    for other in greet:
        pl.semaphore_signal(barrier, inc=1, device_id=other, device_id_type=MESH)

    pairs_in = [
        (blocks_in, blocks),
        (old_in, old),
        (nodes_in, nodes),
        (halos_in, halos),
        (slots_in, slots),
        (weights_in, weights),
        (front_in, front),
        (grads_in, grads),
        (volume_in, volume),
    ]
    arrivals = [pltpu.make_async_copy(src, dst, in_sem.at[i]) for i, (src, dst) in enumerate(pairs_in)]
    for copy in arrivals:
        copy.start()

    arrivals[0].wait()
    arrivals[1].wait()
    pl.semaphore_wait(barrier, len(greet))

    def block_copy(number, theirs, other):
        return pltpu.make_async_remote_copy(
            src_ref=block_out.at[number],
            dst_ref=block_in.at[theirs],
            send_sem=block_send.at[number],
            recv_sem=block_recv.at[theirs],
            device_id=other,
            device_id_type=MESH,
        )

    def pack(number):
        for c in range(CAP):
            rows = old[pl.ds(blocks[number, 0, c], FIELDS, stride=64), :]
            block_out[number, c * FIELDS : (c + 1) * FIELDS, :] = rows

    for peer in peers:
        pack(peer[0])
        block_copy(*peer).start()
    me = 4 + layer
    pack(me)

    arrivals[2].wait()
    arrivals[3].wait()
    for j in range(20):
        spot_idx[j * 4 : (j + 1) * 4, :] = nodes[:, j * LANES : (j + 1) * LANES]
    for k in range(SIDES):
        halo_idx[k * 2 : k * 2 + 2, :] = halos[k] if k < 4 else halos[4 + layer]

    sub = lax.broadcasted_iota(jnp.int32, (8, LANES), 0)
    half = jnp.right_shift(sub, 2)

    def hot_tile(row):
        low = jnp.bitwise_and(jnp.broadcast_to(row, (8, LANES)), LANES - 1)
        return jnp.concatenate([jnp.where(low == sub + g * 8, 1.0, 0.0) for g in range(16)], axis=0).astype(BF16)

    def build_hot(s, carry):
        one_hot[:, lane_tile(s)] = hot_tile(spot_idx[pl.ds(s, 1), :])
        return carry

    def build_halo_hot(s, carry):
        halo_hot[:, lane_tile(s)] = hot_tile(halo_idx[pl.ds(s, 1), :])
        return carry

    lax.fori_loop(0, SPOTS, build_hot, 0, unroll=8)
    lax.fori_loop(0, SIDES * 2, build_halo_hot, 0, unroll=10)

    arrivals[4].wait()
    arrivals[5].wait()
    for j in range(ROWS):
        lookup[pl.ds(j, 4, stride=4), :] = slots[:, j * LANES : (j + 1) * LANES]
        weight_rows[pl.ds(j, 4, stride=4), :] = weights[:, j * LANES : (j + 1) * LANES]

    for copy in arrivals[6:]:
        copy.wait()
    for j in range(5):
        vol_rows[j * 4 : (j + 1) * 4, :] = volume[j]

    lo = [jnp.bitwise_and(lookup[v * 8 : (v + 1) * 8, :], LANES - 1) for v in range(2)]
    blk = [jnp.right_shift(lookup[v * 8 : (v + 1) * 8, :], 7) for v in range(2)]

    def interpolate(source, spot, number, acc):
        acc = list(acc)
        for c in range(CAP):
            hit = [blk[v] == number * CAP + c for v in range(2)]
            for f in range(FIELDS):
                row = jnp.broadcast_to(source[spot, c * FIELDS + f : c * FIELDS + f + 1, :], (8, LANES))
                for v in range(2):
                    acc[f * 2 + v] = jnp.where(hit[v], lane_gather(row, lo[v]), acc[f * 2 + v])
        return acc

    acc = tuple(jnp.zeros((8, LANES), F32) for _ in range(12))
    acc = interpolate(block_out, me, me, acc)
    for number, _, other in [peers[i] for i in (8, 4, 5, 6, 7, 0, 1, 2, 3)]:
        pltpu.make_async_remote_copy(
            src_ref=block_out.at[number],
            dst_ref=block_in.at[number],
            send_sem=block_send.at[number],
            recv_sem=block_recv.at[number],
            device_id=other,
            device_id_type=MESH,
        ).wait_recv()
        acc = interpolate(block_in, number, number, acc)

    for f in range(FIELDS):
        both = acc[f * 2] * weight_rows[0:8, :] + acc[f * 2 + 1] * weight_rows[8:16, :]
        total = both[0:4] + both[4:8]
        if f == 4:
            total = jnp.where(front[...] == 1, ocean_temp, total)
        state[f * 4 : (f + 1) * 4, :] = total
    state[24:32, :] = jnp.zeros((8, LANES), F32)
    tiles = [state[pl.ds(h, 8, stride=4), :] for h in range(ROWS)]

    def halo_copy(k):
        return pltpu.make_async_remote_copy(
            src_ref=halo_out.at[k],
            dst_ref=ghost_in.at[k],
            send_sem=halo_send.at[k],
            recv_sem=halo_recv.at[k],
            device_id=sides[k],
            device_id_type=MESH,
        )

    for k in range(SIDES):
        for r in range(2):
            idx = jnp.broadcast_to(halo_idx[k * 2 + r : k * 2 + r + 1, :], (8, LANES))
            low = jnp.bitwise_and(idx, LANES - 1)
            high = jnp.right_shift(idx, 7)
            kept = jnp.zeros((8, LANES), F32)
            for h in range(ROWS):
                kept = jnp.where(high == h, lane_gather(tiles[h], low), kept)
            halo_out[k, :, r * LANES : (r + 1) * LANES] = kept
        halo_copy(k).start()

    out[0:24, :] = state[0:24, :]

    def look_up(rows, first):
        for t in range(SPOTS // 8):
            at = slice(t * 8, (t + 1) * 8)
            low = jnp.bitwise_and(spot_idx[at, :], LANES - 1)
            high = jnp.right_shift(spot_idx[at, :], 7)
            found = [jnp.zeros((8, LANES), F32) if first else values[f, at, :] for f in range(FIELDS)]
            for code, fetch in rows:
                hit = high == code
                for f in range(FIELDS):
                    row = jnp.broadcast_to(fetch(f), (8, LANES))
                    found[f] = jnp.where(hit, lane_gather(row, low), found[f])
            for f in range(FIELDS):
                values[f, at, :] = found[f]

    look_up([(h, lambda f, h=h: state[f * 4 + h : f * 4 + h + 1, :]) for h in range(ROWS)], True)

    low_x, high_x = x > 0, x < count_x - 1
    low_y, high_y = y > 0, y < count_y - 1
    ghost_live = [low_x, high_x, low_y, high_y]
    back_live = [high_x, low_x, high_y, low_y]
    ghost_rows = []
    for k in range(SIDES):
        for r in range(2):
            code = jnp.where(ghost_live[k], 4 + 2 * k + r, -1) if k < 4 else 4 + 2 * (5 - layer) + r
            ghost_rows.append((code, lambda f, k=k, r=r: ghost_in[k, f : f + 1, r * LANES : (r + 1) * LANES]))
    for k in range(SIDES):
        halo_copy(k).wait_recv()
    look_up(ghost_rows, False)

    for r0 in (0, 8, 12):
        val = [[values[f, pl.ds(r0 * 4 + a, 8, stride=4), :] for a in range(4)] for f in range(FIELDS)]
        grad = [[grads[(3 * a + j) * 20 + r0 : (3 * a + j) * 20 + r0 + 8, :] for j in range(3)] for a in range(4)]
        vol = vol_rows[r0 : r0 + 8, :]
        vg = [[sum(val[i][a] * grad[a][j] for a in range(4)) for j in range(3)] for i in range(3)]
        strain = [[0.5 * (vg[i][j] + vg[j][i]) for j in range(3)] for i in range(3)]
        second = 0.5 * sum(strain[i][j] * strain[i][j] for i in range(3) for j in range(3))
        pm, tm, dm = [0.25 * (val[f][0] + val[f][1] + val[f][2] + val[f][3]) for f in (3, 4, 5)]
        visc2 = (1.0 - dm) * jnp.exp(-tm) * jnp.exp(jnp.log(second + strain_reg) * (-1.0 / 3.0))
        stress = [[visc2 * strain[i][j] - (pm if i == j else 0.0) for j in range(3)] for i in range(3)]
        cont = 0.25 * vol * (vg[0][0] + vg[1][1] + vg[2][2])
        for a in range(4):
            for c in range(4):
                if c < 3:
                    part = vol * sum(stress[c][j] * grad[a][j] for j in range(3))
                    if c == 2:
                        part = part + 0.25 * gravity * vol
                else:
                    part = cont
                for d in range(2):
                    contrib[pl.ds((r0 * 4 + a) * 8 + d * 4 + c, 8, stride=32), :] = part

    acc = jnp.zeros((128, LANES), F32)
    for t in range(SPOTS // 8):
        at = slice(t * 1024, (t + 1) * 1024)
        for u in range(8):
            s = t * 8 + u
            high = jnp.right_shift(jnp.broadcast_to(spot_idx[s : s + 1, :], (8, LANES)), 7) - half
            parts = split_two(contrib[s * 8 : (s + 1) * 8, :])
            hits = [high == 2 * m for m in range(8)]
            rows = [jnp.where(hits[m], parts[part], 0.0) for part in range(2) for m in range(8)]
            left[:, s * LANES : (s + 1) * LANES] = jnp.concatenate(rows, axis=0).astype(BF16)
        acc = acc + lax.dot_general(
            left[:, at], one_hot[:, at], (((1,), (1,)), ((), ())), preferred_element_type=F32
        )
    sums[...] = acc[0:64] + acc[64:128]

    def ret_copy(k):
        return pltpu.make_async_remote_copy(
            src_ref=ret_out.at[k],
            dst_ref=ret_in.at[k],
            send_sem=ret_send.at[k],
            recv_sem=ret_recv.at[k],
            device_id=backs[k],
            device_id_type=MESH,
        )

    for k in range(SIDES):
        ret_out[k] = sums[16 + 8 * k : 24 + 8 * k, :] if k < 4 else jnp.where(layer == 0, sums[56:64, :], sums[48:56, :])
        ret_copy(k).start()

    for k in range(SIDES):
        ret_copy(k).wait_recv()
        for r in range(2):
            u = k * 2 + r
            high = jnp.right_shift(jnp.broadcast_to(halo_idx[u : u + 1, :], (8, LANES)), 7) - half
            if k < 4:
                high = jnp.where(back_live[k], high, -2)
            four = ret_in[k, r * 4 : (r + 1) * 4, :]
            parts = split_two(jnp.concatenate([four, four], axis=0))
            rows = [jnp.where(high == 2 * m, part, 0.0) for part in parts for m in range(2)]
            left_back[:, u * LANES : (u + 1) * LANES] = jnp.concatenate(rows, axis=0).astype(BF16)
    back = lax.dot_general(left_back[...], halo_hot[...], (((1,), (1,)), ((), ())), preferred_element_type=F32)
    out[24:40, :] = sums[0:16, :] + back[0:16] + back[16:32]

    for peer in peers:
        block_copy(*peer).wait_send()
    for k in range(SIDES):
        halo_copy(k).wait_send()
        ret_copy(k).wait_send()


def per_device(old_state, send_blocks, node_slots, node_weights, front_mask, halo_lists, elem_nodes, shape_grads, elem_volume):
    count_x = lax.axis_size("mapx")
    count_y = lax.axis_size("mapy")
    vmem = pl.BlockSpec(memory_space=pltpu.VMEM)
    anywhere = pl.BlockSpec(memory_space=pl.ANY)
    dma = pltpu.SemaphoreType.DMA
    both = pl.pallas_call(
        functools.partial(kernel, count_x, count_y),
        out_shape=jax.ShapeDtypeStruct((40, LANES), F32),
        in_specs=[anywhere] * 9,
        out_specs=vmem,
        scratch_shapes=[
            pltpu.SMEM((10, 1, CAP), jnp.int32),
            pltpu.VMEM((FIELDS * 64, LANES), F32),
            pltpu.VMEM((4, 512), jnp.int32),
            pltpu.VMEM((4, 512), F32),
            pltpu.VMEM((ROWS, LANES), jnp.int32),
            pltpu.VMEM((6, 2, LANES), jnp.int32),
            pltpu.VMEM((4, 2560), jnp.int32),
            pltpu.VMEM((240, LANES), F32),
            pltpu.VMEM((5, 4, LANES), F32),
            pltpu.VMEM((10, CAP * FIELDS, LANES), F32),
            pltpu.VMEM((10, CAP * FIELDS, LANES), F32),
            pltpu.VMEM((16, LANES), jnp.int32),
            pltpu.VMEM((16, LANES), F32),
            pltpu.VMEM((32, LANES), F32),
            pltpu.VMEM((16, LANES), jnp.int32),
            pltpu.VMEM((SIDES, 8, WIDE), F32),
            pltpu.VMEM((SIDES, 8, WIDE), F32),
            pltpu.VMEM((SPOTS, LANES), jnp.int32),
            pltpu.VMEM((LANES, SPOTS * LANES), BF16),
            pltpu.VMEM((LANES, SIDES * WIDE), BF16),
            pltpu.VMEM((FIELDS, SPOTS, LANES), F32),
            pltpu.VMEM((24, LANES), F32),
            pltpu.VMEM((SPOTS * 8, LANES), F32),
            pltpu.VMEM((LANES, SPOTS * LANES), BF16),
            pltpu.VMEM((32, SIDES * WIDE), BF16),
            pltpu.VMEM((64, LANES), F32),
            pltpu.VMEM((SIDES, 8, LANES), F32),
            pltpu.VMEM((SIDES, 8, LANES), F32),
            dma((9,)),
            dma((10,)),
            dma((10,)),
            dma((SIDES,)),
            dma((SIDES,)),
            dma((SIDES,)),
            dma((SIDES,)),
        ],
        compiler_params=pltpu.CompilerParams(collective_id=0, has_side_effects=True),
        name="remap_residual",
    )(
        send_blocks.reshape(10, 1, CAP),
        old_state.reshape(FIELDS * 64, LANES),
        node_slots.reshape(4, 512),
        node_weights.reshape(4, 512),
        front_mask.reshape(ROWS, LANES),
        halo_lists.reshape(6, 2, LANES),
        elem_nodes.reshape(4, 2560),
        shape_grads.reshape(240, LANES),
        elem_volume.reshape(5, 4, LANES),
    )
    new_state = both[0:24].reshape(1, 1, 1, FIELDS, 512)
    residual = both[24:40].reshape(ROWS, 4, LANES).transpose(1, 0, 2).reshape(1, 1, 1, 4, 512)
    return new_state, residual


def solution(mesh):
    deep = P("mapx", "mapy", "layer", None, None)
    flat = P("mapx", "mapy", "layer", None)
    return jax.shard_map(
        per_device,
        mesh=mesh,
        in_specs=(deep, deep, deep, deep, flat, deep, deep, deep, flat),
        out_specs=(deep, deep),
        check_vma=False,
    )
```

time: 46.2 us -> 39.7 us (0.86)
  Pallas kernels: 42.1 us -> 36.1 us
  local copies, waits for them, and re-layouts: 3.2 us -> 2.6 us
    pallas_call x1, Pallas kernels: 42.1 us -> 36.1 us  [per_device(): pl.pallas_call(functools.partial(kernel, count_x, count_y), out_shape=jax...]
    unnamed x7 -> x0, local copies, waits for them, and re-layouts: 3.2 us -> none
    slice x0 -> x2, local copies, waits for them, and re-layouts: none -> 2.6 us  [the longest x1 1.31 us: per_device(): new_state = both[0:24].reshape(1, 1, 1, FIELDS, 512)]
where the time goes in v2:
time: 39.7 us; the launch traced here: 39.4 us
  Pallas kernels  36.1 us (91%)
  local copies, waits for them, and re-layouts  2.6 us (7%)
  between operations  0.64 us (2%)
    pallas_call x1, Pallas kernels, per_device(): pl.pallas_call(functools.partial(kernel, count_x, count_y), out_shape=jax...  36.1 us
    slice x1, local copies, waits for them, and re-layouts, per_device(): new_state = both[0:24].reshape(1, 1, 1, FIELDS, 512)  1.31 us
    slice x1, local copies, waits for them, and re-layouts, per_device(): both[24:40].reshape(ROWS, 4, LANES).transpose(1, 0, 2)  1.3 us

profile of v2, /device:TPU:1, one launch (start us, length us, event | category | flops | bytes accessed | tf_op | source)
XLA Modules:
  0.0 39.4 jit_solution(17834278886871754097)
XLA Ops:
  0.6 36.1 %remap_residual.1 = f32[40,128]{1,0:T(8,128)} custom-call(s32[10,1,16]{2,1,0:T(1,128)} %bitcast.24, f32[384,128]{1,0:T(8,128)} %bitcast.15, s32[4,512]{1,0:T(4,128)} %bitcast.20, f32[4,512]{1,0:T(4,128)} %bitcast.21, s32[4,128]{1,0:T(4,128)} %bitcast.25, s32[6,2,128]{2,1,0:T(2,128)} %bitcast.23, s32[4,2560]{1,0:T(4,128)} %bitcast.17, f32[240,128]{1,0:T(8,128)} %bitcast.16, ...), custom_call_target="tpu_custom_call" | custom-call | tf_op jit(solution)/shard_map/remap_residual/pallas_call | solution.py:347
  36.8 1.3 %slice.7 = f32[16,128]{1,0:T(8,128)} slice(f32[40,128]{1,0:T(8,128)} %remap_residual.1), slice={[24:40], [0:128]} | slice | bytes 16384 | tf_op jit(solution)/shard_map/slice | solution.py:403
  38.1 1.3 %slice.6 = f32[24,128]{1,0:T(8,128)} slice(f32[40,128]{1,0:T(8,128)} %remap_residual.1), slice={[0:24], [0:128]} | slice | bytes 24576 | tf_op jit(solution)/shard_map/slice | solution.py:402

commit v3 on v2

--- a/solution.py
+++ b/solution.py
@@ -146,7 +146,7 @@
     arrivals[2].wait()
     arrivals[3].wait()
     for j in range(20):
-        spot_idx[j * 4 : (j + 1) * 4, :] = nodes[:, j * LANES : (j + 1) * LANES]
+        spot_idx[pl.ds(j, 4, stride=20), :] = nodes[:, j * LANES : (j + 1) * LANES]
     for k in range(SIDES):
         halo_idx[k * 2 : k * 2 + 2, :] = halos[k] if k < 4 else halos[4 + layer]
 
@@ -194,7 +194,7 @@
 
     acc = tuple(jnp.zeros((8, LANES), F32) for _ in range(12))
     acc = interpolate(block_out, me, me, acc)
-    for number, _, other in [peers[i] for i in (8, 4, 5, 6, 7, 0, 1, 2, 3)]:
+    for number, _, other in [peers[i] for i in (8, 0, 1, 2, 3, 4, 5, 6, 7)]:
         pltpu.make_async_remote_copy(
             src_ref=block_out.at[number],
             dst_ref=block_in.at[number],
@@ -266,8 +266,21 @@
         halo_copy(k).wait_recv()
     look_up(ghost_rows, False)
 
-    for r0 in (0, 8, 12):
-        val = [[values[f, pl.ds(r0 * 4 + a, 8, stride=4), :] for a in range(4)] for f in range(FIELDS)]
+    def add_sums(acc, first, last):
+        for s in range(first, last):
+            high = jnp.right_shift(jnp.broadcast_to(spot_idx[s : s + 1, :], (8, LANES)), 7)
+            hits = [high == sub + 8 * m for m in range(2)]
+            parts = [split_two(jnp.broadcast_to(contrib[c, s : s + 1, :], (8, LANES))) for c in range(4)]
+            rows = [jnp.where(hits[m], parts[c][p], 0.0) for p in range(2) for c in range(4) for m in range(2)]
+            left[:, s * LANES : (s + 1) * LANES] = jnp.concatenate(rows, axis=0).astype(BF16)
+        at = slice(first * LANES, last * LANES)
+        return acc + lax.dot_general(
+            left[:, at], one_hot[:, at], (((1,), (1,)), ((), ())), preferred_element_type=F32
+        )
+
+    acc = jnp.zeros((LANES, LANES), F32)
+    for r0, r1 in ((0, 0), (8, 8), (12, 16)):
+        val = [[values[f, a * 20 + r0 : a * 20 + r0 + 8, :] for a in range(4)] for f in range(FIELDS)]
         grad = [[grads[(3 * a + j) * 20 + r0 : (3 * a + j) * 20 + r0 + 8, :] for j in range(3)] for a in range(4)]
         vol = vol_rows[r0 : r0 + 8, :]
         vg = [[sum(val[i][a] * grad[a][j] for a in range(4)) for j in range(3)] for i in range(3)]
@@ -285,22 +298,10 @@
                         part = part + 0.25 * gravity * vol
                 else:
                     part = cont
-                for d in range(2):
-                    contrib[pl.ds((r0 * 4 + a) * 8 + d * 4 + c, 8, stride=32), :] = part
-
-    acc = jnp.zeros((128, LANES), F32)
-    for t in range(SPOTS // 8):
-        at = slice(t * 1024, (t + 1) * 1024)
-        for u in range(8):
-            s = t * 8 + u
-            high = jnp.right_shift(jnp.broadcast_to(spot_idx[s : s + 1, :], (8, LANES)), 7) - half
-            parts = split_two(contrib[s * 8 : (s + 1) * 8, :])
-            hits = [high == 2 * m for m in range(8)]
-            rows = [jnp.where(hits[m], parts[part], 0.0) for part in range(2) for m in range(8)]
-            left[:, s * LANES : (s + 1) * LANES] = jnp.concatenate(rows, axis=0).astype(BF16)
-        acc = acc + lax.dot_general(
-            left[:, at], one_hot[:, at], (((1,), (1,)), ((), ())), preferred_element_type=F32
-        )
+                contrib[c, a * 20 + r0 : a * 20 + r0 + 8, :] = part
+        for a in range(4):
+            acc = add_sums(acc, a * 20 + r1, a * 20 + r0 + 8)
+
     sums[...] = acc[0:64] + acc[64:128]
 
     def ret_copy(k):
@@ -314,7 +315,12 @@
         )
 
     for k in range(SIDES):
-        ret_out[k] = sums[16 + 8 * k : 24 + 8 * k, :] if k < 4 else jnp.where(layer == 0, sums[56:64, :], sums[48:56, :])
+        for r in range(2):
+            row = 4 + 2 * k + r
+            part = sums[pl.ds(row, 4, stride=16), :]
+            if k == 4:
+                part = jnp.where(layer == 0, sums[pl.ds(row + 2, 4, stride=16), :], part)
+            ret_out[k, r * 4 : (r + 1) * 4, :] = part
         ret_copy(k).start()
 
     for k in range(SIDES):
@@ -329,13 +335,20 @@
             rows = [jnp.where(high == 2 * m, part, 0.0) for part in parts for m in range(2)]
             left_back[:, u * LANES : (u + 1) * LANES] = jnp.concatenate(rows, axis=0).astype(BF16)
     back = lax.dot_general(left_back[...], halo_hot[...], (((1,), (1,)), ((), ())), preferred_element_type=F32)
-    out[24:40, :] = sums[0:16, :] + back[0:16] + back[16:32]
+    back = back[0:16] + back[16:32]
+    for h in range(ROWS):
+        out[24 + h * 4 : 28 + h * 4, :] = sums[pl.ds(h, 4, stride=16), :] + back[h * 4 : (h + 1) * 4]
 
     for peer in peers:
         block_copy(*peer).wait_send()
     for k in range(SIDES):
         halo_copy(k).wait_send()
         ret_copy(k).wait_send()
+
+
+def write_outputs(both, out_new, out_res):
+    out_new[...] = both[0:24, :]
+    out_res[...] = both[24:40, :]
 
 
 def per_device(old_state, send_blocks, node_slots, node_weights, front_mask, halo_lists, elem_nodes, shape_grads, elem_volume):
@@ -372,7 +385,7 @@
             pltpu.VMEM((LANES, SIDES * WIDE), BF16),
             pltpu.VMEM((FIELDS, SPOTS, LANES), F32),
             pltpu.VMEM((24, LANES), F32),
-            pltpu.VMEM((SPOTS * 8, LANES), F32),
+            pltpu.VMEM((4, SPOTS, LANES), F32),
             pltpu.VMEM((LANES, SPOTS * LANES), BF16),
             pltpu.VMEM((32, SIDES * WIDE), BF16),
             pltpu.VMEM((64, LANES), F32),
@@ -399,9 +412,15 @@
         shape_grads.reshape(240, LANES),
         elem_volume.reshape(5, 4, LANES),
     )
-    new_state = both[0:24].reshape(1, 1, 1, FIELDS, 512)
-    residual = both[24:40].reshape(ROWS, 4, LANES).transpose(1, 0, 2).reshape(1, 1, 1, 4, 512)
-    return new_state, residual
+    new_state, residual = pl.pallas_call(
+        write_outputs,
+        out_shape=(jax.ShapeDtypeStruct((24, LANES), F32), jax.ShapeDtypeStruct((16, LANES), F32)),
+        in_specs=[vmem],
+        out_specs=(vmem, vmem),
+        name="write_outputs",
+    )(both)
+    residual = residual.reshape(ROWS, 4, LANES).transpose(1, 0, 2)
+    return new_state.reshape(1, 1, 1, FIELDS, 512), residual.reshape(1, 1, 1, 4, 512)
 
 
 def solution(mesh):

time: 39.7 us -> 37.3 us (0.940)
  local copies, waits for them, and re-layouts: 2.6 us -> 0 us
    slice x2 -> x0, local copies, waits for them, and re-layouts: 2.6 us -> none  [the longest x1 1.31 us: per_device(): new_state = both[0:24].reshape(1, 1, 1, FIELDS, 512)]
    pallas_call x0 -> x1, Pallas kernels: none -> 1.33 us  [per_device(): pl.pallas_call(write_outputs, out_shape=(jax.ShapeDtypeStruct((24, LANES)...]
    pallas_call x1, Pallas kernels: 36.1 us -> 35.1 us  [per_device(): pl.pallas_call(functools.partial(kernel, count_x, count_y), out_shape=jax...]
where the time goes in v3:
time: 37.3 us; the launch traced here: 37.1 us
  Pallas kernels  36.4 us (98%)
  between operations  0.64 us (2%)
    pallas_call x1, Pallas kernels, per_device(): pl.pallas_call(functools.partial(kernel, count_x, count_y), out_shape=jax...  35.1 us
    pallas_call x1, Pallas kernels, per_device(): pl.pallas_call(write_outputs, out_shape=(jax.ShapeDtypeStruct((24, LANES)...  1.33 us

profile of v3, /device:TPU:1, one launch (start us, length us, event | category | flops | bytes accessed | tf_op | source)
XLA Modules:
  0.0 37.1 jit_solution(7004594200190615019)
XLA Ops:
  0.6 35.1 %remap_residual.1.both = f32[40,128]{1,0:T(8,128)} custom-call(s32[10,1,16]{2,1,0:T(1,128)} %bitcast.22, f32[384,128]{1,0:T(8,128)} %bitcast.15, s32[4,512]{1,0:T(4,128)} %bitcast.19, f32[4,512]{1,0:T(4,128)} %bitcast.20, s32[4,128]{1,0:T(4,128)} %bitcast.23, s32[6,2,128]{2,1,0:T(2,128)} %bitcast.21, s32[4,2560]{1,0:T(4,128)} %bitcast.17, ...), custom_call_target="tpu_custom_call" | custom-call | tf_op jit(solution)/shard_map/remap_residual/pallas_call | solution.py:360
  35.7 1.3 %write_outputs.1 = (f32[24,128]{1,0:T(8,128)}, f32[16,128]{1,0:T(8,128)}) custom-call(f32[40,128]{1,0:T(8,128)} %remap_residual.1.both), custom_call_target="tpu_custom_call" | custom-call | tf_op jit(solution)/shard_map/write_outputs/pallas_call | solution.py:415

commit v4 on v3

--- a/solution.py
+++ b/solution.py
@@ -48,7 +48,7 @@
     nodes_in,
     grads_in,
     volume_in,
-    out,
+    out_any,
     blocks,
     old,
     slots,
@@ -77,6 +77,7 @@
     sums,
     ret_out,
     ret_in,
+    out,
     in_sem,
     block_send,
     block_recv,
@@ -236,6 +237,8 @@
         halo_copy(k).start()
 
     out[0:24, :] = state[0:24, :]
+    early = pltpu.make_async_copy(out.at[0:24], out_any.at[0:24], in_sem.at[9])
+    early.start()
 
     def look_up(rows, first):
         for t in range(SPOTS // 8):
@@ -257,14 +260,13 @@
     low_y, high_y = y > 0, y < count_y - 1
     ghost_live = [low_x, high_x, low_y, high_y]
     back_live = [high_x, low_x, high_y, low_y]
-    ghost_rows = []
-    for k in range(SIDES):
+    for k in (4, 0, 1, 2, 3):
+        ghost_rows = []
         for r in range(2):
             code = jnp.where(ghost_live[k], 4 + 2 * k + r, -1) if k < 4 else 4 + 2 * (5 - layer) + r
             ghost_rows.append((code, lambda f, k=k, r=r: ghost_in[k, f : f + 1, r * LANES : (r + 1) * LANES]))
-    for k in range(SIDES):
         halo_copy(k).wait_recv()
-    look_up(ghost_rows, False)
+        look_up(ghost_rows, False)
 
     def add_sums(acc, first, last):
         for s in range(first, last):
@@ -339,11 +341,15 @@
     for h in range(ROWS):
         out[24 + h * 4 : 28 + h * 4, :] = sums[pl.ds(h, 4, stride=16), :] + back[h * 4 : (h + 1) * 4]
 
+    late = pltpu.make_async_copy(out.at[24:40], out_any.at[24:40], in_sem.at[10])
+    late.start()
     for peer in peers:
         block_copy(*peer).wait_send()
     for k in range(SIDES):
         halo_copy(k).wait_send()
         ret_copy(k).wait_send()
+    early.wait()
+    late.wait()
 
 
 def write_outputs(both, out_new, out_res):
@@ -355,13 +361,13 @@
     count_x = lax.axis_size("mapx")
     count_y = lax.axis_size("mapy")
     vmem = pl.BlockSpec(memory_space=pltpu.VMEM)
-    anywhere = pl.BlockSpec(memory_space=pl.ANY)
+    far_memory = pl.BlockSpec(memory_space=pltpu.HBM)
     dma = pltpu.SemaphoreType.DMA
     both = pl.pallas_call(
         functools.partial(kernel, count_x, count_y),
         out_shape=jax.ShapeDtypeStruct((40, LANES), F32),
-        in_specs=[anywhere] * 9,
-        out_specs=vmem,
+        in_specs=[far_memory] * 9,
+        out_specs=pl.BlockSpec(memory_space=pl.ANY),
         scratch_shapes=[
             pltpu.SMEM((10, 1, CAP), jnp.int32),
             pltpu.VMEM((FIELDS * 64, LANES), F32),
@@ -391,7 +397,8 @@
             pltpu.VMEM((64, LANES), F32),
             pltpu.VMEM((SIDES, 8, LANES), F32),
             pltpu.VMEM((SIDES, 8, LANES), F32),
-            dma((9,)),
+            pltpu.VMEM((40, LANES), F32),
+            dma((11,)),
             dma((10,)),
             dma((10,)),
             dma((SIDES,)),
@@ -399,24 +406,30 @@
             dma((SIDES,)),
             dma((SIDES,)),
         ],
-        compiler_params=pltpu.CompilerParams(collective_id=0, has_side_effects=True),
+        compiler_params=pltpu.CompilerParams(collective_id=0, has_side_effects=True, vmem_limit_bytes=24 << 20),
         name="remap_residual",
     )(
-        send_blocks.reshape(10, 1, CAP),
-        old_state.reshape(FIELDS * 64, LANES),
-        node_slots.reshape(4, 512),
-        node_weights.reshape(4, 512),
-        front_mask.reshape(ROWS, LANES),
-        halo_lists.reshape(6, 2, LANES),
-        elem_nodes.reshape(4, 2560),
-        shape_grads.reshape(240, LANES),
-        elem_volume.reshape(5, 4, LANES),
+        *(
+            pltpu.with_memory_space_constraint(value, pltpu.HBM)
+            for value in (
+                send_blocks.reshape(10, 1, CAP),
+                old_state.reshape(FIELDS * 64, LANES),
+                node_slots.reshape(4, 512),
+                node_weights.reshape(4, 512),
+                front_mask.reshape(ROWS, LANES),
+                halo_lists.reshape(6, 2, LANES),
+                elem_nodes.reshape(4, 2560),
+                shape_grads.reshape(240, LANES),
+                elem_volume.reshape(5, 4, LANES),
+            )
+        )
     )
     new_state, residual = pl.pallas_call(
         write_outputs,
         out_shape=(jax.ShapeDtypeStruct((24, LANES), F32), jax.ShapeDtypeStruct((16, LANES), F32)),
         in_specs=[vmem],
         out_specs=(vmem, vmem),
+        compiler_params=pltpu.CompilerParams(vmem_limit_bytes=1 << 20),
         name="write_outputs",
     )(both)
     residual = residual.reshape(ROWS, 4, LANES).transpose(1, 0, 2)

time: 37.3 us -> 35.6 us (0.954)
  Pallas kernels: 36.4 us -> 34.8 us
    pallas_call x1, Pallas kernels: 35.1 us -> 34.2 us  [per_device(): pl.pallas_call(functools.partial(kernel, count_x, count_y), out_shape=jax...]
    pallas_call x1, Pallas kernels: 1.33 us -> 0.61 us  [per_device(): pl.pallas_call(write_outputs, out_shape=(jax.ShapeDtypeStruct((24, LANES)...]
where the time goes in v4:
time: 35.6 us; the launch traced here: 35.4 us
  Pallas kernels  34.8 us (98%)
  between operations  0.64 us (2%)
    pallas_call x1, Pallas kernels, per_device(): pl.pallas_call(functools.partial(kernel, count_x, count_y), out_shape=jax...  34.2 us

profile of v4, /device:TPU:1, one launch (start us, length us, event | category | flops | bytes accessed | tf_op | source)
XLA Modules:
  0.0 35.4 jit_solution(15568284492026979564)
XLA Ops:
  0.6 34.2 %remap_residual.1.both = f32[40,128]{1,0:T(8,128)S(1)} custom-call(s32[10,1,16]{2,1,0:T(1,128)} %bitcast.22, f32[384,128]{1,0:T(8,128)} %bitcast.15, s32[4,512]{1,0:T(4,128)} %bitcast.19, f32[4,512]{1,0:T(4,128)} %bitcast.20, s32[4,128]{1,0:T(4,128)} %bitcast.23, s32[6,2,128]{2,1,0:T(2,128)} %bitcast.21, s32[4,2560]{1,0:T(4,128)} %bitcast.17, ...), custom_call_target="tpu_custom_call" | custom-call | tf_op jit(solution)/shard_map/remap_residual/pallas_call | solution.py:366
  34.8 0.6 %write_outputs.1 = (f32[24,128]{1,0:T(8,128)}, f32[16,128]{1,0:T(8,128)}) custom-call(f32[40,128]{1,0:T(8,128)S(1)} %remap_residual.1.both), custom_call_target="tpu_custom_call" | custom-call | tf_op jit(solution)/shard_map/write_outputs/pallas_call | solution.py:427

commit v5 on v4

--- a/solution.py
+++ b/solution.py
@@ -48,7 +48,7 @@
     nodes_in,
     grads_in,
     volume_in,
-    out_any,
+    out,
     blocks,
     old,
     slots,
@@ -77,7 +77,6 @@
     sums,
     ret_out,
     ret_in,
-    out,
     in_sem,
     block_send,
     block_recv,
@@ -121,8 +120,6 @@
 
     arrivals[0].wait()
     arrivals[1].wait()
-    pl.semaphore_wait(barrier, len(greet))
-
     def block_copy(number, theirs, other):
         return pltpu.make_async_remote_copy(
             src_ref=block_out.at[number],
@@ -138,11 +135,12 @@
             rows = old[pl.ds(blocks[number, 0, c], FIELDS, stride=64), :]
             block_out[number, c * FIELDS : (c + 1) * FIELDS, :] = rows
 
+    for number in range(10):
+        pack(number)
+    me = 4 + layer
+    pl.semaphore_wait(barrier, len(greet))
     for peer in peers:
-        pack(peer[0])
         block_copy(*peer).start()
-    me = 4 + layer
-    pack(me)
 
     arrivals[2].wait()
     arrivals[3].wait()
@@ -234,11 +232,10 @@
             for h in range(ROWS):
                 kept = jnp.where(high == h, lane_gather(tiles[h], low), kept)
             halo_out[k, :, r * LANES : (r + 1) * LANES] = kept
+    for k in range(SIDES):
         halo_copy(k).start()
 
     out[0:24, :] = state[0:24, :]
-    early = pltpu.make_async_copy(out.at[0:24], out_any.at[0:24], in_sem.at[9])
-    early.start()
 
     def look_up(rows, first):
         for t in range(SPOTS // 8):
@@ -255,6 +252,9 @@
                 values[f, at, :] = found[f]
 
     look_up([(h, lambda f, h=h: state[f * 4 + h : f * 4 + h + 1, :]) for h in range(ROWS)], True)
+
+    for peer in peers:
+        block_copy(*peer).wait_send()
 
     low_x, high_x = x > 0, x < count_x - 1
     low_y, high_y = y > 0, y < count_y - 1
@@ -323,7 +323,10 @@
             if k == 4:
                 part = jnp.where(layer == 0, sums[pl.ds(row + 2, 4, stride=16), :], part)
             ret_out[k, r * 4 : (r + 1) * 4, :] = part
+    for k in range(SIDES):
         ret_copy(k).start()
+    for k in range(SIDES):
+        halo_copy(k).wait_send()
 
     for k in range(SIDES):
         ret_copy(k).wait_recv()
@@ -341,15 +344,8 @@
     for h in range(ROWS):
         out[24 + h * 4 : 28 + h * 4, :] = sums[pl.ds(h, 4, stride=16), :] + back[h * 4 : (h + 1) * 4]
 
-    late = pltpu.make_async_copy(out.at[24:40], out_any.at[24:40], in_sem.at[10])
-    late.start()
-    for peer in peers:
-        block_copy(*peer).wait_send()
-    for k in range(SIDES):
-        halo_copy(k).wait_send()
+    for k in range(SIDES):
         ret_copy(k).wait_send()
-    early.wait()
-    late.wait()
 
 
 def write_outputs(both, out_new, out_res):
@@ -367,7 +363,7 @@
         functools.partial(kernel, count_x, count_y),
         out_shape=jax.ShapeDtypeStruct((40, LANES), F32),
         in_specs=[far_memory] * 9,
-        out_specs=pl.BlockSpec(memory_space=pl.ANY),
+        out_specs=vmem,
         scratch_shapes=[
             pltpu.SMEM((10, 1, CAP), jnp.int32),
             pltpu.VMEM((FIELDS * 64, LANES), F32),
@@ -397,8 +393,7 @@
             pltpu.VMEM((64, LANES), F32),
             pltpu.VMEM((SIDES, 8, LANES), F32),
             pltpu.VMEM((SIDES, 8, LANES), F32),
-            pltpu.VMEM((40, LANES), F32),
-            dma((11,)),
+            dma((9,)),
             dma((10,)),
             dma((10,)),
             dma((SIDES,)),

time: 35.6 us -> 35.5 us (level)
  no operation moved by 1% of the time
where the time goes in v5:
time: 35.5 us; the launch traced here: 35.4 us
  Pallas kernels  34.8 us (98%)
  between operations  0.64 us (2%)
    pallas_call x1, Pallas kernels, per_device(): pl.pallas_call(functools.partial(kernel, count_x, count_y), out_shape=jax...  34.1 us

profile of v5, /device:TPU:1, one launch (start us, length us, event | category | flops | bytes accessed | tf_op | source)
XLA Modules:
  0.0 35.4 jit_solution(7542805630406911050)
XLA Ops:
  0.6 34.1 %remap_residual.1.both = f32[40,128]{1,0:T(8,128)S(1)} custom-call(s32[10,1,16]{2,1,0:T(1,128)} %bitcast.22, f32[384,128]{1,0:T(8,128)} %bitcast.15, s32[4,512]{1,0:T(4,128)} %bitcast.19, f32[4,512]{1,0:T(4,128)} %bitcast.20, s32[4,128]{1,0:T(4,128)} %bitcast.23, s32[6,2,128]{2,1,0:T(2,128)} %bitcast.21, s32[4,2560]{1,0:T(4,128)} %bitcast.17, ...), custom_call_target="tpu_custom_call" | custom-call | tf_op jit(solution)/shard_map/remap_residual/pallas_call | solution.py:362
  34.8 0.6 %write_outputs.1 = (f32[24,128]{1,0:T(8,128)}, f32[16,128]{1,0:T(8,128)}) custom-call(f32[40,128]{1,0:T(8,128)S(1)} %remap_residual.1.both), custom_call_target="tpu_custom_call" | custom-call | tf_op jit(solution)/shard_map/write_outputs/pallas_call | solution.py:422
